TPU v7x, 256 devices: a whole 4x4x8 slice. The times are simulated.
256 devices in a mesh: atom: 8 (over x, core), ka: 32 (over y, z).
Axes of the slice: x: 4, y: 4, z: 8, core: 2. Of those that a mesh axis runs over, the one named last changes fastest.
Arguments:
- positions: float32 [3, 131072], P(None, 'atom'), may hold values from 0 to 1
- features: bfloat16 [64, 131072], P(None, 'atom'), may hold values from -6 to 6
- species: int32 [131072], P('atom'), may hold values from 0 to 7
- miller: int32 [3, 4096], P(None, 'ka'), may hold values from -8 to 8
- species_table: float32 [64, 8], replicated, may hold values from -6 to 6
- filter_weight: float32 [64, 16], replicated, may hold values from -6 to 6
- norm_gain: float32 [64], replicated, may hold values from 0.25 to 1.75
- up_weight: bfloat16 [256, 64], replicated, may hold values from -0.75 to 0.75
- down_weight: bfloat16 [64, 256], replicated, may hold values from -0.375 to 0.375
Outputs:
- updated: bfloat16 [64, 131072], P(None, ('atom', 'ka'))
All inputs are finite; a program needn't handle non-finite values.
Results may differ from a plain program's by a relative error of at most 0.006.
Values may be sent and summed in bfloat16 or wider, within the bound.
A program may use at most 64 MiB of HBM per device.

v0:
```python
import math

import jax
import jax.numpy as jnp
from jax import lax
from jax.sharding import PartitionSpec as P

K = 4096
NRBF = 16
NSPEC = 8


two_pi = 2.0 * math.pi
k_cutoff = 14.0


def phases(coords, vectors):
    values = vectors.astype(jnp.float32)
    angles = two_pi * (
        coords[0][:, None] * values[0][None, :]
        + coords[1][:, None] * values[1][None, :]
        + coords[2][:, None] * values[2][None, :]
    )
    return (jnp.cos(angles).astype(jnp.bfloat16), jnp.sin(angles).astype(jnp.bfloat16))


def radial_filter(vectors, filter_weight):
    values = vectors.astype(jnp.float32)
    magnitude = jnp.sqrt(values[0] * values[0] + values[1] * values[1] + values[2] * values[2])
    centers = jnp.arange(NRBF, dtype=jnp.float32) * (k_cutoff / (NRBF - 1))
    basis = jnp.exp(-jnp.square((magnitude[None, :] - centers[:, None]) / (k_cutoff / NRBF)))
    return jnp.dot(
        filter_weight, basis, precision=lax.Precision.HIGHEST, preferred_element_type=jnp.float32
    )


def project_back(filtered, cosines, sines):
    dims = (((1,), (1,)), ((), ()))
    first = lax.dot_general(filtered[0], cosines, dims, preferred_element_type=jnp.float32)
    return first + lax.dot_general(filtered[1], sines, dims, preferred_element_type=jnp.float32)


def body(
    positions,
    features,
    species,
    miller,
    species_table,
    filter_weight,
    norm_gain,
    up_weight,
    down_weight,
):
    atoms_here = features.shape[1]
    local_count = atoms_here // lax.axis_size("ka")
    scaling = 1.0 / math.sqrt(atoms_here * lax.axis_size("atom") * K)
    onehot = (species[None, :] == jnp.arange(NSPEC, dtype=jnp.int32)[:, None]).astype(jnp.float32)
    embedded = jnp.dot(
        species_table, onehot, precision=lax.Precision.HIGHEST, preferred_element_type=jnp.float32
    )
    source = (features.astype(jnp.float32) + embedded).astype(jnp.bfloat16)
    cosines, sines = phases(positions, miller)
    real_part = jnp.dot(source, cosines, preferred_element_type=jnp.float32)
    imag_part = jnp.dot(source, sines, preferred_element_type=jnp.float32)
    factors = jnp.stack([real_part, imag_part])
    summed = lax.psum(factors, "atom")
    filtered = (summed * radial_filter(miller, filter_weight)[None] * scaling).astype(jnp.bfloat16)
    ka_index = lax.axis_index("ka")
    local_features = lax.dynamic_slice_in_dim(features, ka_index * local_count, local_count, 1)
    partial_sum = project_back(filtered, cosines, sines)
    message = lax.psum_scatter(partial_sum, "ka", scatter_dimension=1, tiled=True)
    mean_sq = jnp.mean(message * message, axis=0, keepdims=True)
    normed = (message * lax.rsqrt(mean_sq + 1e-06) * norm_gain[:, None]).astype(jnp.bfloat16)
    hidden = jax.nn.silu(jnp.dot(up_weight, normed, preferred_element_type=jnp.float32)).astype(
        jnp.bfloat16
    )
    update = jnp.dot(down_weight, hidden, preferred_element_type=jnp.float32)
    return (local_features.astype(jnp.float32) + update).astype(jnp.bfloat16)


def solution(mesh):
    in_specs = (P(None, "atom"), P(None, "atom"), P("atom"), P(None, "ka"), P(), P(), P(), P(), P())
    out_specs = P(None, ("atom", "ka"))
    return jax.shard_map(body, mesh=mesh, in_specs=in_specs, out_specs=out_specs, check_vma=False)
```

profile of v0, /device:TPU:2, one launch (start us, length us, event | category | flops | bytes accessed | tf_op | source)
XLA Modules:
  0.0 452.1 jit_solution(7611694238206161224)
XLA Ops:
  6.5 0.0 copy-start
  6.5 0.0 all-reduce.2.cloned.1.call-start
  6.5 0.7 convert_element_type.35
  7.2 1.5 fusion.29
  8.7 3.6 fusion.1
  12.3 30.7 %fusion.7 = f32[1,64,128]{2,1,0:T(8,128)S(1)} fusion(bf16[64,16384]{1,0:T(8,128)(2,1)S(1)} %fusion.1, f32[128]{0:T(128)S(1)} %get-tuple-element.9, f32[16384]{0:T(1024)S(1)} %bitcast.61, f32[128]{0:T(128)S(1)} %get-tuple-element.10, f32[16384]{0:T(1024)S(1)} %bitcast.65, f32[128]{0:T(128)S(1)} %get-tuple-element.11, f32[16384]{0:T(1024)S(1)} %bitcast.57), kind=kOutput, calls=%fused_computation.14 | convolution fusion | flops 283115520 | bytes 2328064 | tf_op jit(solution)/shard_map/dot_general | solution.py:63
  43.0 0.0 copy-start.2
  43.0 31.2 %fusion.8 = f32[1,64,128]{2,1,0:T(8,128)S(1)} fusion(bf16[64,16384]{1,0:T(8,128)(2,1)S(1)} %fusion.1, f32[128]{0:T(128)S(1)} %get-tuple-element.9, f32[16384]{0:T(1024)S(1)} %bitcast.62, f32[128]{0:T(128)S(1)} %get-tuple-element.10, f32[16384]{0:T(1024)S(1)} %bitcast.66, f32[128]{0:T(128)S(1)} %get-tuple-element.11, f32[16384]{0:T(1024)S(1)} %bitcast.58), kind=kOutput, calls=%fused_computation.15 | convolution fusion | flops 283115520 | bytes 2328064 | tf_op jit(solution)/shard_map/dot_general | solution.py:64
  74.2 0.6 pad_maximum_fusion
  74.9 0.0 all-reduce.2.cloned.1.call-update
  74.9 0.0 reduce-scatter.2.cloned.1.call-start
  75.0 0.0 copy-done.2
  75.0 0.2 convolution_bitcast_fusion.3
  75.2 65.4 %all-reduce.2.cloned.1.call-done = f32[2,64,128]{2,1,0:T(8,128)} async-done(((f32[2,64,128]{2,1,0:T(8,128)}), f32[2,64,128]{2,1,0:T(8,128)}) %all-reduce.2.cloned.1.call-update) | async-done | bytes 65552 | tf_op jit(solution)/shard_map/psum | solution.py:66
  140.6 0.8 multiply_convert_fusion.4
  141.5 41.2 %fusion.3 = f32[64,16384]{1,0:T(8,128)S(1)} fusion(f32[128]{0:T(128)S(1)} %get-tuple-element.9, f32[16384]{0:T(1024)S(1)} %bitcast.63, f32[128]{0:T(128)S(1)} %get-tuple-element.10, f32[16384]{0:T(1024)S(1)} %bitcast.67, f32[128]{0:T(128)S(1)} %get-tuple-element.11, f32[16384]{0:T(1024)S(1)} %bitcast.59, bf16[2,64,128]{2,1,0:T(8,128)(2,1)S(1)} %multiply_convert_fusion.4), kind=kOutput, calls=%fused_computation.8 | convolution fusion | flops 283115520 | bytes 4408832 | tf_op jit(solution)/shard_map/dot_general | solution.py:39
  182.8 34.3 %convolution_add_fusion = f32[64,16384]{1,0:T(8,128)} fusion(f32[64,16384]{1,0:T(8,128)S(1)} %fusion.3, f32[128]{0:T(128)S(1)} %get-tuple-element.9, f32[16384]{0:T(1024)S(1)} %bitcast.64, f32[128]{0:T(128)S(1)} %get-tuple-element.10, f32[16384]{0:T(1024)S(1)} %bitcast.68, f32[128]{0:T(128)S(1)} %get-tuple-element.11, f32[16384]{0:T(1024)S(1)} %bitcast.60, ...), kind=kOutput, calls=%fused_computation | convolution fusion | flops 284164096 | bytes 8603136 | tf_op jit(solution)/shard_map/dot_general | solution.py:40
  217.1 0.0 copy-start.1
  217.1 0.0 copy-start.3
  217.1 0.0 reduce-scatter.2.cloned.1.call-update
  217.1 224.9 %reduce-scatter.2.cloned.1.call-done = f32[64,512]{1,0:T(8,128)} async-done(((f32[64,16384]{1,0:T(8,128)}), f32[64,512]{1,0:T(8,128)}) %reduce-scatter.2.cloned.1.call-update) | async-done | bytes 131088 | tf_op jit(solution)/shard_map/reduce_scatter | solution.py:71
  442.0 0.9 multiply_reduce_fusion
  442.9 0.0 copy-done
  442.9 0.0 copy-done.1
  442.9 0.0 copy-done.3
  442.9 2.1 fusion.6
  (3 shorter events, 0.0 us)
Async XLA Ops:
  6.5 436.4 %copy-start = (bf16[64,256]{1,0:T(8,128)(2,1)S(1)}, bf16[64,256]{1,0:T(8,128)(2,1)}, u32[]{:S(2)}) copy-start(bf16[64,256]{1,0:T(8,128)(2,1)} %param.17) | copy-start | bytes 98308
  6.5 134.1 %all-reduce.2.cloned.1.call-start = ((), (), s32[]{:S(2)}) async-start(), calls=%async_computation.1 | async-start | bytes 131072 | tf_op jit(solution)/shard_map/psum | solution.py:66
  43.0 32.0 %copy-start.2 = (f32[64,16]{0,1:T(8,128)S(1)}, f32[64,16]{0,1:T(8,128)}, u32[]{:S(2)}) copy-start(f32[64,16]{0,1:T(8,128)} %param.14) | copy-start | bytes 12292
  74.9 367.1 %reduce-scatter.2.cloned.1.call-start = ((), (), s32[]{:S(2)}) async-start(), calls=%async_computation.2 | async-start | bytes 4325376 | tf_op jit(solution)/shard_map/reduce_scatter | solution.py:71
  217.1 225.8 %copy-start.1 = (bf16[256,64]{0,1:T(8,128)(2,1)S(1)}, bf16[256,64]{0,1:T(8,128)(2,1)}, u32[]{:S(2)}) copy-start(bf16[256,64]{0,1:T(8,128)(2,1)} %param.16) | copy-start | bytes 98308
  217.1 225.9 %copy-start.3 = (f32[64]{0:T(128)S(1)}, f32[64]{0:T(128)}, u32[]{:S(2)}) copy-start(f32[64]{0:T(128)} %param.15) | copy-start | bytes 772
Sparse Core Ops, SparseCore 0:
  75.0 65.5 all-reduce.1
  217.2 224.6 reduce-scatter.1
where the time goes:
time: 460 us; the launch traced here: 452 us
  waiting for transfers between devices  290 us (63%)
  matrix products  143 us (31%)
  between operations  13.7 us (3%)
    reduce_scatter x1, waiting for transfers between devices, body(): lax.psum_scatter(partial_sum, 'ka', scatter_dimension=1, tiled=True)  225 us
    psum x1, waiting for transfers between devices, body(): summed = lax.psum(factors, 'atom')  65.4 us
    dot_general x1, matrix products, project_back(): lax.dot_general(filtered[0], cosines, dims, preferred_element_type=jnp.fl...  41.2 us
    dot_general x1, matrix products, project_back(): lax.dot_general(filtered[1], sines, dims, preferred_element_type=jnp.floa...  34.3 us
    dot_general x1, matrix products, body(): imag_part = jnp.dot(source, sines, preferred_element_type=jnp.float32)  31.2 us
    dot_general x1, matrix products, body(): real_part = jnp.dot(source, cosines, preferred_element_type=jnp.float32)  30.7 us
  transfers between devices with their start and end apart: 2, of which 2 were waited for; matrix products, arithmetic and copies ran while one was open for 0% of the time, Pallas kernels for 0%

commit v1 on v0

v1 whole, which is shorter than its diff:
```python
import functools
import math

import jax
import jax.numpy as jnp
from jax import lax
from jax.experimental import pallas as pl
from jax.experimental.pallas import tpu as pltpu
from jax.sharding import PartitionSpec as P

MESH = pl.DeviceIdType.MESH
F32, BF16 = jnp.float32, jnp.bfloat16
NRBF = 16
NSPEC = 8
MAXM = 8
XYR = 304
LW = 384
CHUNK = 512
K_CUTOFF = 14.0

def _fit():
    import numpy as np

    n = 400
    u = 0.125 + 0.125 * np.cos(np.pi * (np.arange(n) + 0.5) / n)
    r = np.sqrt(u)
    c = np.polynomial.chebyshev.Chebyshev.fit(u, np.cos(2 * np.pi * r), 5, domain=[0, 0.25])
    s = np.polynomial.chebyshev.Chebyshev.fit(u, np.sin(2 * np.pi * r) / r, 5, domain=[0, 0.25])
    return (
        [float(v) for v in c.convert(kind=np.polynomial.Polynomial).coef],
        [float(v) for v in s.convert(kind=np.polynomial.Polynomial).coef],
    )


COS_COEF, SIN_COEF = _fit()


def poly(u, coef):
    acc = jnp.full_like(u, coef[-1])
    for c in coef[-2::-1]:
        acc = acc * u + c
    return acc


def harmonics(row, orders):
    t = row * orders
    r = t - jnp.round(t)
    u = r * r
    return poly(u, COS_COEF), r * poly(u, SIN_COEF)


def iota(shape, axis):
    return lax.broadcasted_iota(jnp.int32, shape, axis)


def lane_orders(tile, shape, axis):
    lane = iota(shape, axis)
    low = lane & 7
    if tile < 2:
        ta = jnp.full(shape, tile, jnp.int32)
        p = (lane >> 4) + 1
        tb = (lane >> 3) & 1
        q = low + 1
        return ta, p, tb, q, lane >= 0
    odd = (lane >> 3) & 1
    in_x, in_y = lane < 16, (lane >= 16) & (lane < 32)
    zero = jnp.zeros(shape, jnp.int32)
    ta = jnp.where(in_x, odd, zero)
    p = jnp.where(in_x, low + 1, zero)
    tb = jnp.where(in_y, odd, zero)
    q = jnp.where(in_y, low + 1, zero)
    return ta, p, tb, q, lane < 33


def swap8(x):
    lane = iota(x.shape, 1)
    return jnp.where((lane & 8) == 0, pltpu.roll(x, 120, 1), pltpu.roll(x, 8, 1))


def tiles_of(x):
    return [x[:, 128 * t : 128 * (t + 1)] for t in range(3)]


def partners(g):
    s = [swap8(t) for t in g]
    lane = iota(g[0].shape, 1)
    zero = jnp.zeros_like(g[0])
    la = [g[1], g[0], jnp.where(lane < 16, s[2], zero)]
    lb = [s[0], s[1], jnp.where((lane >= 16) & (lane < 32), s[2], zero)]
    return la, lb, [s[1], s[0], zero]


def body_kernel(
    sizes,
    pos_ref,
    feat_hbm,
    species_ref,
    miller_ref,
    tab_ref,
    fw_ref,
    gain_ref,
    up_ref,
    down_ref,
    out_ref,
    feat_blk,
    feat_loc,
    xy,
    zz,
    gacc,
    gsend,
    grecv,
    mil_all,
    codes,
    wacc,
    hmat,
    msgs,
    mrecv,
    mflat,
    local_sem,
    mil_send,
    mil_recv,
    g_send,
    g_recv,
    m_send,
    m_recv,
):
    n_atom, n_ka, atoms, scaling = sizes
    ia, ik = lax.axis_index("atom"), lax.axis_index("ka")
    local = atoms // n_ka
    n_chunks = atoms // CHUNK

    block = pltpu.make_async_copy(
        feat_hbm.at[pl.ds(pl.multiple_of((ik // 4) * 8, 8), 8), :], feat_blk, local_sem.at[0]
    )
    block.start()
    mine = pltpu.make_async_copy(
        feat_hbm.at[:, pl.ds(pl.multiple_of(ik * local, local), local)], feat_loc, local_sem.at[1]
    )
    mine.start()

    barrier = pltpu.get_barrier_semaphore()

    def greet_ka(d, _):
        pl.semaphore_signal(barrier, inc=1, device_id=(ia, lax.rem(ik + d, n_ka)), device_id_type=MESH)
        return 0

    lax.fori_loop(1, n_ka, greet_ka, 0)

    def greet_atom(d, _):
        pl.semaphore_signal(barrier, inc=1, device_id=(lax.rem(ia + d, n_atom), ik), device_id_type=MESH)
        return 0

    lax.fori_loop(1, n_atom, greet_atom, 0)

    mil_all[ik] = jnp.concatenate(
        [miller_ref[...].astype(F32), jnp.zeros((5, 128), F32)], axis=0
    )

    pl.semaphore_wait(barrier, n_ka - 1 + n_atom - 1)

    def mil_copy(slot, to):
        return pltpu.make_async_remote_copy(
            src_ref=mil_all.at[ik],
            dst_ref=mil_all.at[slot],
            send_sem=mil_send.at[to],
            recv_sem=mil_recv.at[slot],
            device_id=(ia, to),
            device_id_type=MESH,
        )

    def send_miller(d, _):
        mil_copy(ik, lax.rem(ik + d, n_ka)).start()
        return 0

    lax.fori_loop(1, n_ka, send_miller, 0)

    sub = iota((8, CHUNK), 0)
    orders = (sub + 1).astype(F32)
    first_row = sub == 0
    tabs = []
    for c in range(2):
        t = jnp.zeros((8, CHUNK), F32)
        for sp in range(NSPEC):
            t = jnp.where(sub == sp, tab_ref[2 * ik + c, sp], t)
        tabs.append(t)
    which = [sub == lax.rem(2 * ik, 8) + c for c in range(2)]
    gacc[...] = jnp.zeros_like(gacc)
    block.wait()

    def gather_chunk(j, _):
        cols = pl.ds(pl.multiple_of(j * CHUNK, CHUNK), CHUNK)
        xc, xs = harmonics(jnp.broadcast_to(pos_ref[0:1, cols], (8, CHUNK)), orders)
        yc, ys = harmonics(jnp.broadcast_to(pos_ref[1:2, cols], (8, CHUNK)), orders)
        zc, zs = harmonics(jnp.broadcast_to(pos_ref[2:3, cols], (8, CHUNK)), orders)
        zz[0:8, cols] = zc
        zz[8:16, cols] = zs
        for half, xx in enumerate((xc, xs)):
            for a in range(8):
                xa = jnp.broadcast_to(xx[a : a + 1, :], (8, CHUNK))
                r0 = 16 * (8 * half + a)
                xy[r0 : r0 + 16, cols] = jnp.concatenate([xa * yc, xa * ys], axis=0).astype(BF16)
        xy[256:272, cols] = jnp.concatenate([xc, xs], axis=0).astype(BF16)
        xy[272:288, cols] = jnp.concatenate([yc, ys], axis=0).astype(BF16)
        one = jnp.where(first_row, 1.0, 0.0)
        xy[288:304, cols] = jnp.concatenate([one, jnp.zeros_like(one)], axis=0).astype(BF16)
        fb = feat_blk[:, cols].astype(F32)
        spc = jnp.broadcast_to(species_ref[0:1, cols], (8, CHUNK))
        hot = spc == sub
        rows, extra = [], []
        for c in range(2):
            s = jnp.where(which[c], fb, 0.0) + jnp.where(hot, tabs[c], 0.0)
            s = jnp.broadcast_to(jnp.sum(s, axis=0, keepdims=True), (8, CHUNK))
            s = s.astype(BF16).astype(F32)
            rows += [s * zc, s * zs]
            extra.append(jnp.where(first_row, s, 0.0))
        sz = jnp.concatenate(rows + extra, axis=0).astype(BF16)
        gacc[0:XYR, 0:48] += lax.dot_general(
            xy[:, cols], sz, (((1,), (1,)), ((), ())), preferred_element_type=F32
        )
        return 0

    lax.fori_loop(0, n_chunks, gather_chunk, 0)

    gt = gacc[...].T[0:48, :]
    gsend[...] = gt.astype(BF16)

    def g_copy(slot, to):
        return pltpu.make_async_remote_copy(
            src_ref=gsend,
            dst_ref=grecv.at[slot],
            send_sem=g_send.at[to],
            recv_sem=g_recv.at[slot],
            device_id=(to, ik),
            device_id_type=MESH,
        )

    def send_g(d, _):
        g_copy(ia, lax.rem(ia + d, n_atom)).start()
        return 0

    lax.fori_loop(1, n_atom, send_g, 0)

    for t in range(3):
        n = min(128, XYR - 128 * t)
        _, p, _, q, used = lane_orders(t, (128, 128), 0)
        codes[128 * t : 128 * t + n, :] = jnp.where(used, p * 9 + q, -1).astype(F32)[0:n, :]
    wacc[...] = jnp.zeros_like(wacc)
    sub1 = iota((8, 128), 0)
    r8 = (sub1 + 1).astype(F32)
    top = sub1 == 0

    def wait_miller(d, _):
        mil_copy(lax.rem(ik + d, n_ka), ik).wait_recv()
        return 0

    lax.fori_loop(1, n_ka, wait_miller, 0)

    def count_block(j, _):
        m = mil_all[j]
        mx, my, mz = [jnp.broadcast_to(m[i : i + 1, :], (8, 128)) for i in range(3)]
        gx, gy, gz = [jnp.where(v < 0, -1.0, 1.0) for v in (mx, my, mz)]
        code = jnp.abs(mx) * 9.0 + jnp.abs(my)
        hot_xy = jnp.where(
            codes[...] == jnp.broadcast_to(code[0:1, :], (XYR, 128)), 1.0, 0.0
        ).astype(BF16)
        az = jnp.abs(mz)
        hz = jnp.where(az == r8, 1.0, 0.0)
        h0 = jnp.where((az == 0.0) & top, 1.0, 0.0)
        wr = jnp.concatenate(
            [hz, hz * (gy * gz), hz * (gx * gz), hz * (gx * gy), h0, h0 * (gx * gy)], axis=0
        ).astype(BF16)
        wacc[0:XYR, 0:48] += lax.dot_general(
            hot_xy, wr, (((1,), (1,)), ((), ())), preferred_element_type=F32
        )
        return 0

    lax.fori_loop(0, n_ka, count_block, 0)
    wt = wacc[...].T
    w_plain, w_yz, w_xz, w_xy, w_plain0, w_xy0 = [
        tiles_of(wt[8 * i : 8 * i + 8, :]) for i in range(6)
    ]

    signs, radials, radials0 = [], [], []
    for t in range(3):
        ta, p, tb, q, _ = lane_orders(t, (8, 128), 1)
        signs.append((ta, tb))
        pq = (p * p + q * q).astype(F32)
        per_channel = []
        for mag in (jnp.sqrt(pq + r8 * r8), jnp.sqrt(pq)):
            acc = [jnp.zeros((8, 128), F32) for _ in range(2)]
            for b in range(NRBF):
                z = (mag - b * (K_CUTOFF / (NRBF - 1))) / (K_CUTOFF / NRBF)
                e = jnp.exp(-(z * z))
                for c in range(2):
                    acc[c] = acc[c] + fw_ref[2 * ik + c, b] * e
            per_channel.append([v * scaling for v in acc])
        radials.append(per_channel[0])
        radials0.append(per_channel[1])

    def wait_g(d, _):
        g_copy(lax.rem(ia + d, n_atom), ia).wait_recv()
        return 0

    lax.fori_loop(1, n_atom, wait_g, 0)
    grecv[ia] = gsend[...]
    g = grecv[0].astype(F32)
    for i in range(1, n_atom):
        g = g + grecv[i].astype(F32)

    rows = []
    for c in range(2):
        gz = [tiles_of(g[16 * c + 8 * tz : 16 * c + 8 * tz + 8, :]) for tz in range(2)]
        swapped = [partners(v) for v in gz]
        for tz in range(2):
            la, lb, _ = swapped[1 - tz]
            _, _, lab = swapped[tz]
            out = []
            for t in range(3):
                ta, tb = signs[t]
                u = jnp.where(tb == tz, -lb[t], lb[t]) * w_yz[t]
                v = jnp.where(ta == tz, -la[t], la[t]) * w_xz[t]
                w = jnp.where(ta == tb, -lab[t], lab[t]) * w_xy[t]
                out.append((gz[tz][t] * w_plain[t] + u + v + w) * radials[t][c])
            rows.append(jnp.concatenate(out, axis=1))
    for c in range(2):
        g0 = tiles_of(g[32 + 8 * c : 40 + 8 * c, :])
        _, _, lab = partners(g0)
        out = []
        for t in range(3):
            ta, tb = signs[t]
            w = jnp.where(ta == tb, -lab[t], lab[t]) * w_xy0[t]
            out.append((g0[t] * w_plain0[t] + w) * radials0[t][c])
        rows.append(jnp.concatenate(out, axis=1))
    hmat[...] = jnp.concatenate(rows, axis=0).astype(BF16)

    def m_copy(slot, to):
        return pltpu.make_async_remote_copy(
            src_ref=msgs.at[to],
            dst_ref=mrecv.at[slot],
            send_sem=m_send.at[to],
            recv_sem=m_recv.at[slot],
            device_id=(ia, to),
            device_id_type=MESH,
        )

    def message_of(j):
        cols = pl.ds(pl.multiple_of(j * CHUNK, CHUNK), CHUNK)
        d = jnp.dot(hmat[:, 0:XYR], xy[:, cols], preferred_element_type=F32)
        zc, zs = zz[0:8, cols], zz[8:16, cols]
        parts = []
        for c in range(2):
            s = d[16 * c : 16 * c + 8, :] * zc + d[16 * c + 8 : 16 * c + 16, :] * zs
            s = s + d[32 + 8 * c : 40 + 8 * c, :]
            s = jnp.sum(s, axis=0, keepdims=True)
            parts += [s[:, 128 * i : 128 * (i + 1)] for i in range(CHUNK // 128)]
        return jnp.concatenate(parts, axis=0).astype(BF16)

    def send_message(d, _):
        j = lax.rem(ik + d, n_ka)
        msgs[j] = message_of(j)
        m_copy(ik, j).start()
        return 0

    lax.fori_loop(1, n_ka, send_message, 0)
    mrecv[ik] = message_of(ik)

    mine.wait()

    def wait_message(d, _):
        m_copy(lax.rem(ik + d, n_ka), ik).wait_recv()
        return 0

    lax.fori_loop(1, n_ka, wait_message, 0)

    mflat[...] = mrecv[...].astype(F32).reshape(mflat.shape)
    message = jnp.concatenate(
        [mflat[pl.ds(i, 64, stride=4), :] for i in range(local // 128)], axis=1
    )
    eye = iota((64, 64), 0) == iota((64, 64), 1)
    gain = jnp.sum(jnp.where(eye, jnp.broadcast_to(gain_ref[...], (64, 64)), 0.0), axis=1, keepdims=True)
    mean_sq = jnp.sum(message * message, axis=0, keepdims=True) * (1.0 / 64.0)
    normed = (message * lax.rsqrt(mean_sq + 1e-06) * gain).astype(BF16)
    hidden = jnp.dot(up_ref[...], normed, preferred_element_type=F32)
    hidden = (hidden / (1.0 + jnp.exp(-hidden))).astype(BF16)
    update = jnp.dot(down_ref[...], hidden, preferred_element_type=F32)
    out_ref[...] = (feat_loc[...].astype(F32) + update).astype(BF16)

    def drain_ka(d, _):
        to = lax.rem(ik + d, n_ka)
        mil_copy(ik, to).wait_send()
        m_copy(ik, to).wait_send()
        return 0

    lax.fori_loop(1, n_ka, drain_ka, 0)

    def drain_atom(d, _):
        g_copy(ia, lax.rem(ia + d, n_atom)).wait_send()
        return 0

    lax.fori_loop(1, n_atom, drain_atom, 0)


def solution(mesh):
    n_atom, n_ka = mesh.shape["atom"], mesh.shape["ka"]

    def body(positions, features, species, miller, species_table, filter_weight, norm_gain, up_weight, down_weight):
        channels, atoms = features.shape
        local = atoms // n_ka
        n_vectors = miller.shape[1] * n_ka
        scaling = 1.0 / math.sqrt(atoms * n_atom * n_vectors)
        vmem = pl.BlockSpec(memory_space=pltpu.VMEM)
        smem = pl.BlockSpec(memory_space=pltpu.SMEM)
        return pl.pallas_call(
            functools.partial(body_kernel, (n_atom, n_ka, atoms, scaling)),
            out_shape=jax.ShapeDtypeStruct((channels, local), BF16),
            in_specs=[vmem, pl.BlockSpec(memory_space=pl.ANY), vmem, vmem, smem, smem, vmem, vmem, vmem],
            out_specs=vmem,
            scratch_shapes=[
                pltpu.VMEM((8, atoms), BF16),
                pltpu.VMEM((channels, local), BF16),
                pltpu.VMEM((XYR, atoms), BF16),
                pltpu.VMEM((16, atoms), F32),
                pltpu.VMEM((LW, 128), F32),
                pltpu.VMEM((48, LW), BF16),
                pltpu.VMEM((n_atom, 48, LW), BF16),
                pltpu.VMEM((n_ka, 8, 128), F32),
                pltpu.VMEM((XYR, 128), F32),
                pltpu.VMEM((LW, 128), F32),
                pltpu.VMEM((48, LW), BF16),
                pltpu.VMEM((n_ka, 8, 128), BF16),
                pltpu.VMEM((n_ka, 8, 128), BF16),
                pltpu.VMEM((n_ka * 8, 128), F32),
                pltpu.SemaphoreType.DMA((2,)),
                pltpu.SemaphoreType.DMA((n_ka,)),
                pltpu.SemaphoreType.DMA((n_ka,)),
                pltpu.SemaphoreType.DMA((n_atom,)),
                pltpu.SemaphoreType.DMA((n_atom,)),
                pltpu.SemaphoreType.DMA((n_ka,)),
                pltpu.SemaphoreType.DMA((n_ka,)),
            ],
            compiler_params=pltpu.CompilerParams(
                collective_id=0, has_side_effects=True, vmem_limit_bytes=60 * 1024 * 1024
            ),
            name="ewald",
        )(
            positions,
            features,
            species.reshape(1, atoms),
            miller,
            species_table,
            filter_weight,
            norm_gain.reshape(1, channels),
            up_weight,
            down_weight,
        )

    in_specs = (P(None, "atom"), P(None, "atom"), P("atom"), P(None, "ka"), P(), P(), P(), P(), P())
    out_specs = P(None, ("atom", "ka"))
    return jax.shard_map(body, mesh=mesh, in_specs=in_specs, out_specs=out_specs, check_vma=False)
```

time: 460 us -> 47 us (0.10)
  the two profiles are of different devices: /device:TPU:2 before, /device:TPU:1 now
where the time goes in v1:
time: 47 us; the launch traced here: 46.6 us
  Pallas kernels  40.9 us (87%)
  local copies, waits for them, and re-layouts  5.71 us (12%)
    pallas_call x1, Pallas kernels, body(): pl.pallas_call(functools.partial(body_kernel, (n_atom, n_ka, atoms, scali...  40.9 us
    unnamed x4, local copies, waits for them, and re-layouts  5.71 us

profile of v1, /device:TPU:1, one launch (start us, length us, event | category | flops | bytes accessed | tf_op | source)
XLA Modules:
  0.0 46.6 jit_solution(11589636692348333767)
XLA Ops:
  0.0 1.4 %copy.10.tab_ref = f32[64,8]{1,0:T(8,128)} copy(f32[64,8]{0,1:T(8,128)} %param.13) | data formatting | bytes 4096 | tf_op args[4]
  1.4 1.4 %copy.11.fw_ref = f32[64,16]{1,0:T(8,128)} copy(f32[64,16]{0,1:T(8,128)} %param.14) | data formatting | bytes 8192 | tf_op args[5]
  2.8 1.5 %copy.12.up_ref = bf16[256,64]{1,0:T(8,128)(2,1)} copy(bf16[256,64]{0,1:T(8,128)(2,1)} %param.16) | data formatting | bytes 65536 | tf_op args[7]
  4.2 40.9 %ewald.1 = bf16[64,512]{1,0:T(8,128)(2,1)} custom-call(f32[3,16384]{1,0:T(4,128)} %pos_ref.1, bf16[64,16384]{1,0:T(8,128)(2,1)} %feat_hbm.1, s32[1,16384]{1,0:T(1,128)} %bitcast.2, s32[3,128]{1,0:T(4,128)} %miller_ref.1, f32[64,8]{1,0:T(8,128)} %copy.10.tab_ref, f32[64,16]{1,0:T(8,128)} %copy.11.fw_ref, f32[1,64]{1,0:T(1,128)} %bitcast.3, ...), custom_call_target="tpu_custom_call" | custom-call | tf_op jit(solution)/shard_map/ewald/pallas_call | solution.py:413
  45.2 1.5 %copy.14 = bf16[64,512]{1,0:T(8,128)(2,1)} copy(bf16[64,512]{1,0:T(8,128)(2,1)} %ewald.1) | data formatting | bytes 131072

commit v2 on v1

v2 whole, which is shorter than its diff:
```python
import functools
import math

import jax
import jax.numpy as jnp
from jax import lax
from jax.experimental import pallas as pl
from jax.experimental.pallas import tpu as pltpu
from jax.sharding import PartitionSpec as P

MESH = pl.DeviceIdType.MESH
F32, BF16 = jnp.float32, jnp.bfloat16
NRBF = 16
NSPEC = 8
MAXM = 8
XYR = 304
LW = 384
CHUNK = 512
K_CUTOFF = 14.0

def _fit():
    import numpy as np

    n = 400
    u = 0.125 + 0.125 * np.cos(np.pi * (np.arange(n) + 0.5) / n)
    r = np.sqrt(u)
    c = np.polynomial.chebyshev.Chebyshev.fit(u, np.cos(2 * np.pi * r), 4, domain=[0, 0.25])
    s = np.polynomial.chebyshev.Chebyshev.fit(u, np.sin(2 * np.pi * r) / r, 4, domain=[0, 0.25])
    return (
        [float(v) for v in c.convert(kind=np.polynomial.Polynomial).coef],
        [float(v) for v in s.convert(kind=np.polynomial.Polynomial).coef],
    )


COS_COEF, SIN_COEF = _fit()


def poly(u, coef):
    acc = jnp.full_like(u, coef[-1])
    for c in coef[-2::-1]:
        acc = acc * u + c
    return acc


def harmonics(row, orders):
    t = row * orders
    r = t - jnp.round(t)
    u = r * r
    return poly(u, COS_COEF), r * poly(u, SIN_COEF)


def iota(shape, axis):
    return lax.broadcasted_iota(jnp.int32, shape, axis)


def lane_orders(tile, shape, axis):
    lane = iota(shape, axis)
    low = lane & 7
    if tile < 2:
        ta = jnp.full(shape, tile, jnp.int32)
        p = (lane >> 4) + 1
        tb = (lane >> 3) & 1
        q = low + 1
        return ta, p, tb, q, lane >= 0
    odd = (lane >> 3) & 1
    in_x, in_y = lane < 16, (lane >= 16) & (lane < 32)
    zero = jnp.zeros(shape, jnp.int32)
    ta = jnp.where(in_x, odd, zero)
    p = jnp.where(in_x, low + 1, zero)
    tb = jnp.where(in_y, odd, zero)
    q = jnp.where(in_y, low + 1, zero)
    return ta, p, tb, q, lane < 33


def swap8(x):
    lane = iota(x.shape, 1)
    return jnp.where((lane & 8) == 0, pltpu.roll(x, 120, 1), pltpu.roll(x, 8, 1))


def tiles_of(x):
    return [x[:, 128 * t : 128 * (t + 1)] for t in range(3)]


def partners(g):
    s = [swap8(t) for t in g]
    lane = iota(g[0].shape, 1)
    zero = jnp.zeros_like(g[0])
    la = [g[1], g[0], jnp.where(lane < 16, s[2], zero)]
    lb = [s[0], s[1], jnp.where((lane >= 16) & (lane < 32), s[2], zero)]
    return la, lb, [s[1], s[0], zero]


GROUP = 4


def body_kernel(
    sizes,
    pos_hbm,
    feat_hbm,
    species_hbm,
    miller_hbm,
    tab_hbm,
    fw_hbm,
    gain_hbm,
    up_hbm,
    down_hbm,
    out_ref,
    pos_ref,
    species_ref,
    miller_ref,
    tab_ref,
    fw_ref,
    gain_ref,
    up_ref,
    down_ref,
    feat_blk,
    feat_loc,
    xy,
    sz,
    zz,
    xrows,
    gacc,
    gsend,
    grecv,
    mil_all,
    hmat,
    msgs,
    mrecv,
    mflat,
    local_sem,
    mil_send,
    mil_recv,
    g_send,
    g_recv,
    m_send,
    m_recv,
):
    n_atom, n_ka, ny, nz, atoms, scaling = sizes
    ia, ik = lax.axis_index("atom"), lax.axis_index("ka")
    local = atoms // n_ka
    n_chunks = atoms // CHUNK
    n_vec = n_ka * 128

    barrier = pltpu.get_barrier_semaphore()

    def greet_ka(d, _):
        pl.semaphore_signal(barrier, inc=1, device_id=(ia, lax.rem(ik + d, n_ka)), device_id_type=MESH)
        return 0

    def greet_atom(d, _):
        pl.semaphore_signal(barrier, inc=1, device_id=(lax.rem(ia + d, n_atom), ik), device_id_type=MESH)
        return 0

    loads = []
    for i, (src, dst) in enumerate(
        [
            (pos_hbm, pos_ref),
            (species_hbm, species_ref),
            (feat_hbm.at[pl.ds(pl.multiple_of((ik // 4) * 8, 8), 8), :], feat_blk),
            (tab_hbm, tab_ref),
            (miller_hbm, miller_ref),
            (fw_hbm, fw_ref),
            (gain_hbm, gain_ref),
            (up_hbm, up_ref),
            (down_hbm, down_ref),
            (feat_hbm.at[:, pl.ds(pl.multiple_of(ik * local, local), local)], feat_loc),
        ]
    ):
        copy = pltpu.make_async_copy(src, dst, local_sem.at[i])
        copy.start()
        loads.append(copy)
    lax.fori_loop(1, n_ka, greet_ka, 0)
    lax.fori_loop(1, n_atom, greet_atom, 0)

    first = pl.ds(0, CHUNK)
    xy[:, first] = jnp.zeros((XYR, CHUNK), BF16)
    sz[:, first] = jnp.zeros((48, CHUNK), BF16)
    gacc[...] = jnp.zeros_like(gacc)

    sub = iota((8, CHUNK), 0)
    orders = (sub + 1).astype(F32)
    for copy in loads[:5]:
        copy.wait()
    mil_all[:, pl.ds(pl.multiple_of(ik * 128, 128), 128)] = jnp.concatenate(
        [miller_ref[...].astype(F32), jnp.zeros((5, 128), F32)], axis=0
    )
    column = iota((NSPEC, 64), 1)
    tabs = [
        jnp.broadcast_to(
            jnp.sum(jnp.where(column == 2 * ik + c, tab_ref[...], 0.0), axis=1, keepdims=True), (8, CHUNK)
        )
        for c in range(2)
    ]
    which = [sub == lax.rem(2 * ik, 8) + c for c in range(2)]

    def products(j):
        cols = pl.ds(pl.multiple_of(j * CHUNK, CHUNK), CHUNK)
        return lax.dot_general(
            sz[:, cols], xy[:, cols], (((1,), (1,)), ((), ())), preferred_element_type=F32
        )

    def gather_chunk(j, _):
        part = products(jnp.maximum(j - 1, 0))
        cols = pl.ds(pl.multiple_of(j * CHUNK, CHUNK), CHUNK)
        xc, xs = harmonics(jnp.broadcast_to(pos_ref[0:1, cols], (8, CHUNK)), orders)
        xrows[0:8, :] = xc
        xrows[8:16, :] = xs
        yc, ys = harmonics(jnp.broadcast_to(pos_ref[1:2, cols], (8, CHUNK)), orders)
        y16 = jnp.concatenate([yc, ys], axis=0).astype(BF16)
        zc, zs = harmonics(jnp.broadcast_to(pos_ref[2:3, cols], (8, CHUNK)), orders)
        zz[0:8, cols] = zc
        zz[8:16, cols] = zs
        z16 = jnp.concatenate([zc, zs], axis=0).astype(BF16)
        for a in range(16):
            xa = jnp.broadcast_to(xrows[a : a + 1, :], (8, CHUNK))
            xy[16 * a : 16 * a + 16, cols] = jnp.concatenate([xa, xa], axis=0).astype(BF16) * y16
        xy[256:272, cols] = jnp.concatenate([xc, xs], axis=0).astype(BF16)
        xy[272:288, cols] = y16
        one = jnp.where(sub == 0, 1.0, 0.0)
        xy[288:304, cols] = jnp.concatenate([one, jnp.zeros_like(one)], axis=0).astype(BF16)
        fb = feat_blk[:, cols].astype(F32)
        hot = jnp.broadcast_to(species_ref[0:1, cols], (8, CHUNK)) == sub
        extra = jnp.zeros((8, CHUNK), F32)
        for c in range(2):
            s = jnp.where(which[c], fb, 0.0) + jnp.where(hot, tabs[c], 0.0)
            s = jnp.broadcast_to(jnp.sum(s, axis=0, keepdims=True), (8, CHUNK))
            extra = jnp.where(sub == c, s, extra)
            sz[16 * c : 16 * c + 16, cols] = jnp.concatenate([s, s], axis=0).astype(BF16) * z16
        sz[32:48, cols] = jnp.concatenate([extra, jnp.zeros_like(extra)], axis=0).astype(BF16)
        gacc[:, 0:XYR] += part
        return 0

    lax.fori_loop(0, n_chunks, gather_chunk, 0)
    gacc[:, 0:XYR] += products(n_chunks - 1)
    gsend[...] = gacc[0:40, :].astype(BF16)

    pl.semaphore_wait(barrier, n_ka - 1 + n_atom - 1)

    def g_copy(slot, to):
        return pltpu.make_async_remote_copy(
            src_ref=gsend,
            dst_ref=grecv.at[slot],
            send_sem=g_send,
            recv_sem=g_recv,
            device_id=(to, ik),
            device_id_type=MESH,
        )

    def send_g(d, _):
        g_copy(ia, lax.rem(ia + d, n_atom)).start()
        return 0

    def mil_copy(ref, dst, to):
        return pltpu.make_async_remote_copy(
            src_ref=ref, dst_ref=dst, send_sem=mil_send, recv_sem=mil_recv, device_id=(ia, to), device_id_type=MESH
        )

    own = mil_all.at[:, pl.ds(pl.multiple_of(ik * 128, 128), 128)]

    def farther(k, n):
        return n // 2 + (1 - 2 * lax.rem(k, 2)) * ((k + 1) // 2)

    def partner(i):
        dz, dy = farther(i // ny, nz), farther(lax.rem(i, ny), ny)
        y, z = lax.rem(ik // nz + dy, ny), lax.rem(lax.rem(ik, nz) + dz, nz)
        return y * nz + z

    def send_miller(i, _):
        mil_copy(own, own, partner(i)).start()
        return 0

    lax.fori_loop(0, n_ka - 1, send_miller, 0)
    lax.fori_loop(1, n_atom, send_g, 0)

    for copy in loads[5:]:
        copy.wait()
    sub1 = iota((8, 128), 0)
    r8 = (sub1 + 1).astype(F32)
    column = iota((NRBF, 64), 1)
    weights = [
        jnp.sum(jnp.where(column == 2 * ik + c, fw_ref[...], 0.0), axis=1, keepdims=True) * scaling
        for c in range(2)
    ]
    signs, radials, radials0 = [], [], []
    for t in range(3):
        ta, p, tb, q, _ = lane_orders(t, (8, 128), 1)
        signs.append((ta, tb))
        pq = (p * p + q * q).astype(F32)
        per_channel = []
        for mag in (jnp.sqrt(pq + r8 * r8), jnp.sqrt(pq)):
            acc = [jnp.zeros((8, 128), F32) for _ in range(2)]
            for b in range(NRBF):
                z = (mag - b * (K_CUTOFF / (NRBF - 1))) * (NRBF / K_CUTOFF)
                e = jnp.exp(-(z * z))
                for c in range(2):
                    acc[c] = acc[c] + weights[c][b : b + 1, :] * e
            per_channel.append(acc)
        radials.append(per_channel[0])
        radials0.append(jnp.where(sub1 == 0, per_channel[1][0], per_channel[1][1]))

    expand = []
    row = iota((96, 128), 0)
    for t in range(3):
        _, p, _, q, used = lane_orders(t, (96, 128), 1)
        expand.append(jnp.where(used & (row == p * 9 + q), 1.0, 0.0))
    expand = jnp.concatenate(expand, axis=1).astype(BF16)

    mil_copy(mil_all.at[:, 0 : n_vec - 128], mil_all.at[:, 0 : n_vec - 128], ik).wait_recv()
    codes = iota((96, CHUNK), 0).astype(F32)
    counts = jnp.zeros((48, 96), F32)
    for j in range(n_vec // CHUNK):
        m = mil_all[:, CHUNK * j : CHUNK * (j + 1)]
        mx, my, mz = [jnp.broadcast_to(m[i : i + 1, :], (8, CHUNK)) for i in range(3)]
        gx, gy, gz = [jnp.where(v < 0, -1.0, 1.0) for v in (mx, my, mz)]
        code = jnp.abs(mx) * 9.0 + jnp.abs(my)
        hot_xy = jnp.where(codes == jnp.broadcast_to(code[0:1, :], (96, CHUNK)), 1.0, 0.0).astype(BF16)
        az = jnp.abs(mz)
        hz = jnp.where(az == orders, 1.0, 0.0)
        h0 = jnp.where((az == 0.0) & (sub < 2), 1.0, 0.0)
        wr = jnp.concatenate(
            [hz, hz * (gy * gz), hz * (gx * gz), hz * (gx * gy), h0, h0 * (gx * gy)], axis=0
        ).astype(BF16)
        counts = counts + lax.dot_general(
            wr, hot_xy, (((1,), (1,)), ((), ())), preferred_element_type=F32
        )
    high = jnp.floor(counts * (1.0 / 256.0))
    low = counts - 256.0 * high
    wt = 256.0 * jnp.dot(high.astype(BF16), expand, preferred_element_type=F32) + jnp.dot(
        low.astype(BF16), expand, preferred_element_type=F32
    )
    w_plain, w_yz, w_xz, w_xy, w_plain0, w_xy0 = [
        tiles_of(wt[8 * i : 8 * i + 8, :]) for i in range(6)
    ]

    pltpu.make_async_remote_copy(
        src_ref=grecv.at[0 : n_atom - 1],
        dst_ref=grecv.at[0 : n_atom - 1],
        send_sem=g_send,
        recv_sem=g_recv,
        device_id=(ia, ik),
        device_id_type=MESH,
    ).wait_recv()
    grecv[ia] = gsend[...]
    g = grecv[0].astype(F32)
    for i in range(1, n_atom):
        g = g + grecv[i].astype(F32)

    rows = []
    for c in range(2):
        gz = [tiles_of(g[16 * c + 8 * tz : 16 * c + 8 * tz + 8, :]) for tz in range(2)]
        swapped = [partners(v) for v in gz]
        for tz in range(2):
            la, lb, _ = swapped[1 - tz]
            _, _, lab = swapped[tz]
            out = []
            for t in range(3):
                ta, tb = signs[t]
                u = jnp.where(tb == tz, -lb[t], lb[t]) * w_yz[t]
                v = jnp.where(ta == tz, -la[t], la[t]) * w_xz[t]
                w = jnp.where(ta == tb, -lab[t], lab[t]) * w_xy[t]
                out.append((gz[tz][t] * w_plain[t] + u + v + w) * radials[t][c])
            rows.append(jnp.concatenate(out, axis=1))
    g0 = tiles_of(g[32:40, :])
    _, _, lab = partners(g0)
    out = []
    for t in range(3):
        ta, tb = signs[t]
        w = jnp.where(ta == tb, -lab[t], lab[t]) * w_xy0[t]
        out.append((g0[t] * w_plain0[t] + w) * radials0[t])
    rows.append(jnp.concatenate(out, axis=1))
    rows.append(jnp.zeros((8, LW), F32))
    hmat[...] = jnp.concatenate(rows, axis=0).astype(BF16)

    def m_copy(slot, to):
        return pltpu.make_async_remote_copy(
            src_ref=msgs.at[to],
            dst_ref=mrecv.at[slot],
            send_sem=m_send,
            recv_sem=m_recv,
            device_id=(ia, to),
            device_id_type=MESH,
        )

    def message_of(d, cols):
        zc, zs = zz[0:8, cols], zz[8:16, cols]
        parts = []
        for c in range(2):
            s = d[16 * c : 16 * c + 8, :] * zc + d[16 * c + 8 : 16 * c + 16, :] * zs
            s = s + jnp.where(sub == c, d[32:40, :], 0.0)
            s = jnp.sum(s, axis=0, keepdims=True)
            parts += [s[:, 128 * i : 128 * (i + 1)] for i in range(CHUNK // 128)]
        return jnp.concatenate(parts, axis=0).astype(BF16)

    def send_messages(i, _):
        to = [partner(GROUP * i + k) for k in range(GROUP)]
        cols = [pl.ds(pl.multiple_of(j * CHUNK, CHUNK), CHUNK) for j in to]
        ds = [jnp.dot(hmat[:, 0:XYR], xy[:, c], preferred_element_type=F32) for c in cols]
        for k in range(GROUP):
            msgs[to[k]] = message_of(ds[k], cols[k])
        for k in range(GROUP):
            @pl.when(to[k] != ik)
            def _():
                m_copy(ik, to[k]).start()
        return 0

    lax.fori_loop(0, n_ka // GROUP, send_messages, 0)
    mrecv[ik] = msgs[ik]
    eye = iota((64, 64), 0) == iota((64, 64), 1)
    gain = jnp.sum(jnp.where(eye, jnp.broadcast_to(gain_ref[...], (64, 64)), 0.0), axis=1, keepdims=True)

    def all_messages():
        return pltpu.make_async_remote_copy(
            src_ref=mrecv.at[0 : n_ka - 1],
            dst_ref=mrecv.at[0 : n_ka - 1],
            send_sem=m_send,
            recv_sem=m_recv,
            device_id=(ia, ik),
            device_id_type=MESH,
        )

    all_messages().wait_recv()

    mflat[...] = mrecv[...].astype(F32).reshape(mflat.shape)
    message = jnp.concatenate(
        [mflat[pl.ds(i, 64, stride=4), :] for i in range(local // 128)], axis=1
    )
    mean_sq = jnp.sum(message * message, axis=0, keepdims=True) * (1.0 / 64.0)
    normed = (message * lax.rsqrt(mean_sq + 1e-06) * gain).astype(BF16)
    hidden = lax.dot_general(up_ref[...], normed, (((0,), (0,)), ((), ())), preferred_element_type=F32)
    hidden = (hidden / (1.0 + jnp.exp(-hidden))).astype(BF16)
    update = jnp.dot(down_ref[...], hidden, preferred_element_type=F32)
    out_ref[...] = (feat_loc[...].astype(F32) + update).astype(BF16)

    mil_copy(mil_all.at[:, 0 : n_vec - 128], mil_all.at[:, 0 : n_vec - 128], ik).wait_send()
    all_messages().wait_send()
    pltpu.make_async_remote_copy(
        src_ref=grecv.at[0 : n_atom - 1],
        dst_ref=grecv.at[0 : n_atom - 1],
        send_sem=g_send,
        recv_sem=g_recv,
        device_id=(ia, ik),
        device_id_type=MESH,
    ).wait_send()


def solution(mesh):
    n_atom, n_ka = mesh.shape["atom"], mesh.shape["ka"]
    ny, nz = 4, n_ka // 4

    def body(positions, features, species, miller, species_table, filter_weight, norm_gain, up_weight, down_weight):
        channels, atoms = features.shape
        local = atoms // n_ka
        n_vectors = miller.shape[1] * n_ka
        hid = up_weight.shape[0]
        scaling = 1.0 / math.sqrt(atoms * n_atom * n_vectors)
        any_space = pl.BlockSpec(memory_space=pl.ANY)
        return pl.pallas_call(
            functools.partial(body_kernel, (n_atom, n_ka, ny, nz, atoms, scaling)),
            out_shape=jax.ShapeDtypeStruct((channels, local), BF16),
            in_specs=[any_space] * 9,
            out_specs=pl.BlockSpec(memory_space=pltpu.VMEM),
            scratch_shapes=[
                pltpu.VMEM((3, atoms), F32),
                pltpu.VMEM((1, atoms), jnp.int32),
                pltpu.VMEM((3, 128), jnp.int32),
                pltpu.VMEM((NSPEC, channels), F32),
                pltpu.VMEM((NRBF, channels), F32),
                pltpu.VMEM((1, channels), F32),
                pltpu.VMEM((channels, hid), BF16),
                pltpu.VMEM((channels, hid), BF16),
                pltpu.VMEM((8, atoms), BF16),
                pltpu.VMEM((channels, local), BF16),
                pltpu.VMEM((XYR, atoms), BF16),
                pltpu.VMEM((48, atoms), BF16),
                pltpu.VMEM((16, atoms), F32),
                pltpu.VMEM((16, CHUNK), F32),
                pltpu.VMEM((48, LW), F32),
                pltpu.VMEM((40, LW), BF16),
                pltpu.VMEM((n_atom, 40, LW), BF16),
                pltpu.VMEM((8, n_vectors), F32),
                pltpu.VMEM((48, LW), BF16),
                pltpu.VMEM((n_ka, 8, 128), BF16),
                pltpu.VMEM((n_ka, 8, 128), BF16),
                pltpu.VMEM((n_ka * 8, 128), F32),
                pltpu.SemaphoreType.DMA((10,)),
                pltpu.SemaphoreType.DMA,
                pltpu.SemaphoreType.DMA,
                pltpu.SemaphoreType.DMA,
                pltpu.SemaphoreType.DMA,
                pltpu.SemaphoreType.DMA,
                pltpu.SemaphoreType.DMA,
            ],
            compiler_params=pltpu.CompilerParams(
                collective_id=0, has_side_effects=True, vmem_limit_bytes=24 * 1024 * 1024
            ),
            name="ewald",
        )(
            positions,
            features,
            species.reshape(1, atoms),
            miller,
            species_table.T,
            filter_weight.T,
            norm_gain.reshape(1, channels),
            up_weight.T,
            down_weight,
        )

    in_specs = (P(None, "atom"), P(None, "atom"), P("atom"), P(None, "ka"), P(), P(), P(), P(), P())
    out_specs = P(None, ("atom", "ka"))
    return jax.shard_map(body, mesh=mesh, in_specs=in_specs, out_specs=out_specs, check_vma=False)
```

time: 47 us -> 38.7 us (0.82)
  Pallas kernels: 40.9 us -> 30 us
  local copies, waits for them, and re-layouts: 5.71 us -> 8.24 us
    pallas_call x1, Pallas kernels: 40.9 us -> 30 us  [body(): pl.pallas_call(functools.partial(body_kernel, (n_atom, n_ka, ny, nz, atom...]
    unnamed x4 -> x19, local copies, waits for them, and re-layouts: 5.71 us -> 8.24 us
where the time goes in v2:
time: 38.7 us; the launch traced here: 38.3 us
  Pallas kernels  30 us (78%)
  local copies, waits for them, and re-layouts  8.24 us (21%)
    pallas_call x1, Pallas kernels, body(): pl.pallas_call(functools.partial(body_kernel, (n_atom, n_ka, ny, nz, atom...  30 us
    unnamed x19, local copies, waits for them, and re-layouts  8.24 us

profile of v2, /device:TPU:1, one launch (start us, length us, event | category | flops | bytes accessed | tf_op | source)
XLA Modules:
  0.0 38.3 jit_solution(9012790632297007257)
XLA Ops:
  0.0 0.0 copy-start
  0.0 1.6 %copy-done = bf16[64,16384]{1,0:T(8,128)(2,1)S(1)} copy-done((bf16[64,16384]{1,0:T(8,128)(2,1)S(1)}, bf16[64,16384]{1,0:T(8,128)(2,1)}, u32[]{:S(2)}) %copy-start) | copy-done | bytes 2097176
  1.6 0.0 copy-start.1
  1.6 0.9 %copy-done.1 = f32[3,16384]{1,0:T(4,128)S(1)} copy-done((f32[3,16384]{1,0:T(4,128)S(1)}, f32[3,16384]{1,0:T(4,128)}, u32[]{:S(2)}) %copy-start.1) | copy-done | bytes 196632
  2.5 0.0 copy-start.2
  2.5 0.8 %copy-done.2 = s32[16384]{0:T(1024)S(1)} copy-done((s32[16384]{0:T(1024)S(1)}, s32[16384]{0:T(1024)}, u32[]{:S(2)}) %copy-start.2) | copy-done | bytes 65560
  3.4 0.0 copy-start.3
  3.4 0.8 %copy-done.3 = bf16[256,64]{0,1:T(8,128)(2,1)S(1)} copy-done((bf16[256,64]{0,1:T(8,128)(2,1)S(1)}, bf16[256,64]{0,1:T(8,128)(2,1)}, u32[]{:S(2)}) %copy-start.3) | copy-done | bytes 32792
  4.1 0.0 copy-start.4
  4.1 0.8 %copy-done.4 = bf16[64,256]{1,0:T(8,128)(2,1)S(1)} copy-done((bf16[64,256]{1,0:T(8,128)(2,1)S(1)}, bf16[64,256]{1,0:T(8,128)(2,1)}, u32[]{:S(2)}) %copy-start.4) | copy-done | bytes 32792
  4.9 0.0 copy-start.5
  4.9 0.7 %copy-done.5 = f32[64,16]{0,1:T(8,128)S(1)} copy-done((f32[64,16]{0,1:T(8,128)S(1)}, f32[64,16]{0,1:T(8,128)}, u32[]{:S(2)}) %copy-start.5) | copy-done | bytes 4120
  5.6 0.0 copy-start.6
  5.6 0.7 %copy-done.6 = f32[64,8]{0,1:T(8,128)S(1)} copy-done((f32[64,8]{0,1:T(8,128)S(1)}, f32[64,8]{0,1:T(8,128)}, u32[]{:S(2)}) %copy-start.6) | copy-done | bytes 2072
  6.3 0.0 copy-start.7
  6.3 0.7 %copy-done.7 = s32[3,128]{1,0:T(4,128)S(1)} copy-done((s32[3,128]{1,0:T(4,128)S(1)}, s32[3,128]{1,0:T(4,128)}, u32[]{:S(2)}) %copy-start.7) | copy-done | bytes 1560
  7.0 0.0 copy-start.8
  7.0 0.7 %copy-done.8 = f32[64]{0:T(128)S(1)} copy-done((f32[64]{0:T(128)S(1)}, f32[64]{0:T(128)}, u32[]{:S(2)}) %copy-start.8) | copy-done | bytes 280
  7.6 30.0 %ewald.1 = bf16[64,512]{1,0:T(8,128)(2,1)S(1)} custom-call(f32[3,16384]{1,0:T(4,128)S(1)} %copy-done.1, bf16[64,16384]{1,0:T(8,128)(2,1)S(1)} %copy-done, s32[1,16384]{1,0:T(1,128)S(1)} %bitcast.5, s32[3,128]{1,0:T(4,128)S(1)} %copy-done.7, f32[8,64]{1,0:T(8,128)S(1)} %bitcast.8, f32[16,64]{1,0:T(8,128)S(1)} %bitcast.7, f32[1,64]{1,0:T(1,128)S(1)} %bitcast.9, ...), custom_call_target="tpu_custom_call" | custom-call | tf_op jit(solution)/shard_map/ewald/pallas_call | solution.py:457
  37.6 0.6 %copy.11 = bf16[64,512]{1,0:T(8,128)(2,1)} copy(bf16[64,512]{1,0:T(8,128)(2,1)S(1)} %ewald.1) | data formatting | bytes 131072
Async XLA Ops:
  0.0 1.6 %copy-start = (bf16[64,16384]{1,0:T(8,128)(2,1)S(1)}, bf16[64,16384]{1,0:T(8,128)(2,1)}, u32[]{:S(2)}) copy-start(bf16[64,16384]{1,0:T(8,128)(2,1)} %feat_hbm.1) | copy-start | bytes 6291460
  1.6 0.9 %copy-start.1 = (f32[3,16384]{1,0:T(4,128)S(1)}, f32[3,16384]{1,0:T(4,128)}, u32[]{:S(2)}) copy-start(f32[3,16384]{1,0:T(4,128)} %pos_hbm.1) | copy-start | bytes 589828
  2.5 0.8 %copy-start.2 = (s32[16384]{0:T(1024)S(1)}, s32[16384]{0:T(1024)}, u32[]{:S(2)}) copy-start(s32[16384]{0:T(1024)} %param.11) | copy-start | bytes 196612
  3.4 0.8 %copy-start.3 = (bf16[256,64]{0,1:T(8,128)(2,1)S(1)}, bf16[256,64]{0,1:T(8,128)(2,1)}, u32[]{:S(2)}) copy-start(bf16[256,64]{0,1:T(8,128)(2,1)} %param.16) | copy-start | bytes 98308
  4.1 0.8 %copy-start.4 = (bf16[64,256]{1,0:T(8,128)(2,1)S(1)}, bf16[64,256]{1,0:T(8,128)(2,1)}, u32[]{:S(2)}) copy-start(bf16[64,256]{1,0:T(8,128)(2,1)} %down_hbm.1) | copy-start | bytes 98308
  4.9 0.7 %copy-start.5 = (f32[64,16]{0,1:T(8,128)S(1)}, f32[64,16]{0,1:T(8,128)}, u32[]{:S(2)}) copy-start(f32[64,16]{0,1:T(8,128)} %param.14) | copy-start | bytes 12292
  5.6 0.7 %copy-start.6 = (f32[64,8]{0,1:T(8,128)S(1)}, f32[64,8]{0,1:T(8,128)}, u32[]{:S(2)}) copy-start(f32[64,8]{0,1:T(8,128)} %param.13) | copy-start | bytes 6148
  6.3 0.7 %copy-start.7 = (s32[3,128]{1,0:T(4,128)S(1)}, s32[3,128]{1,0:T(4,128)}, u32[]{:S(2)}) copy-start(s32[3,128]{1,0:T(4,128)} %miller_hbm.1) | copy-start | bytes 4612
  7.0 0.7 %copy-start.8 = (f32[64]{0:T(128)S(1)}, f32[64]{0:T(128)}, u32[]{:S(2)}) copy-start(f32[64]{0:T(128)} %param.15) | copy-start | bytes 772

commit v3 on v2

--- a/solution.py
+++ b/solution.py
@@ -453,7 +453,7 @@
         n_vectors = miller.shape[1] * n_ka
         hid = up_weight.shape[0]
         scaling = 1.0 / math.sqrt(atoms * n_atom * n_vectors)
-        any_space = pl.BlockSpec(memory_space=pl.ANY)
+        any_space = pl.BlockSpec(memory_space=pltpu.HBM)
         return pl.pallas_call(
             functools.partial(body_kernel, (n_atom, n_ka, ny, nz, atoms, scaling)),
             out_shape=jax.ShapeDtypeStruct((channels, local), BF16),
@@ -494,7 +494,7 @@
                 collective_id=0, has_side_effects=True, vmem_limit_bytes=24 * 1024 * 1024
             ),
             name="ewald",
-        )(
+        )(*[pltpu.with_memory_space_constraint(v, pltpu.HBM) for v in (
             positions,
             features,
             species.reshape(1, atoms),
@@ -504,7 +504,7 @@
             norm_gain.reshape(1, channels),
             up_weight.T,
             down_weight,
-        )
+        )])
 
     in_specs = (P(None, "atom"), P(None, "atom"), P("atom"), P(None, "ka"), P(), P(), P(), P(), P())
     out_specs = P(None, ("atom", "ka"))

time: 38.7 us -> 30.9 us (0.80)
  local copies, waits for them, and re-layouts: 8.24 us -> 0.63 us
    unnamed x19 -> x1, local copies, waits for them, and re-layouts: 8.24 us -> 0.63 us
where the time goes in v3:
time: 30.9 us; the launch traced here: 30.8 us
  Pallas kernels  30.2 us (98%)
  local copies, waits for them, and re-layouts  0.63 us (2%)
    pallas_call x1, Pallas kernels, body(): pl.pallas_call(functools.partial(body_kernel, (n_atom, n_ka, ny, nz, atom...  30.2 us
    unnamed x1, local copies, waits for them, and re-layouts  0.63 us

profile of v3, /device:TPU:1, one launch (start us, length us, event | category | flops | bytes accessed | tf_op | source)
XLA Modules:
  0.0 30.8 jit_solution(4116576651676004703)
XLA Ops:
  0.0 30.2 %ewald.1 = bf16[64,512]{1,0:T(8,128)(2,1)S(1)} custom-call(f32[3,16384]{1,0:T(4,128)} %pos_hbm.1, bf16[64,16384]{1,0:T(8,128)(2,1)} %feat_hbm.1, s32[1,16384]{1,0:T(1,128)} %bitcast.5, s32[3,128]{1,0:T(4,128)} %miller_hbm.1, f32[8,64]{1,0:T(8,128)} %bitcast.8, f32[16,64]{1,0:T(8,128)} %bitcast.7, f32[1,64]{1,0:T(1,128)} %bitcast.9, bf16[64,256]{1,0:T(8,128)(2,1)} %bitcast.6, ...), custom_call_target="tpu_custom_call" | custom-call | tf_op jit(solution)/shard_map/ewald/pallas_call | solution.py:457
  30.2 0.6 %copy.11 = bf16[64,512]{1,0:T(8,128)(2,1)} copy(bf16[64,512]{1,0:T(8,128)(2,1)S(1)} %ewald.1) | data formatting | bytes 131072

commit v4 on v3

--- a/solution.py
+++ b/solution.py
@@ -13,8 +13,9 @@
 NRBF = 16
 NSPEC = 8
 MAXM = 8
-XYR = 304
-LW = 384
+LW = 128
+SR = 112
+GR = 104
 CHUNK = 512
 K_CUTOFF = 14.0
 
@@ -53,41 +54,32 @@
     return lax.broadcasted_iota(jnp.int32, shape, axis)
 
 
-def lane_orders(tile, shape, axis):
+def lane_orders(shape, axis):
     lane = iota(shape, axis)
-    low = lane & 7
-    if tile < 2:
-        ta = jnp.full(shape, tile, jnp.int32)
-        p = (lane >> 4) + 1
-        tb = (lane >> 3) & 1
-        q = low + 1
-        return ta, p, tb, q, lane >= 0
-    odd = (lane >> 3) & 1
-    in_x, in_y = lane < 16, (lane >= 16) & (lane < 32)
-    zero = jnp.zeros(shape, jnp.int32)
-    ta = jnp.where(in_x, odd, zero)
-    p = jnp.where(in_x, low + 1, zero)
-    tb = jnp.where(in_y, odd, zero)
-    q = jnp.where(in_y, low + 1, zero)
-    return ta, p, tb, q, lane < 33
-
-
-def swap8(x):
+    main = lane < 112
+    u = jnp.where(main, lane >> 4, lane - 112)
+    tu = jnp.where((u >= 3) & (u < 6), 1, 0)
+    a = jnp.where(u < 3, u + 1, jnp.where(u < 6, u - 2, 0))
+    ty = jnp.where(main, (lane >> 3) & 1, 0)
+    q = jnp.where(main, (lane & 7) + 1, 0)
+    return tu, a, ty, q, lane < 119
+
+
+def swap_y(x):
     lane = iota(x.shape, 1)
-    return jnp.where((lane & 8) == 0, pltpu.roll(x, 120, 1), pltpu.roll(x, 8, 1))
-
-
-def tiles_of(x):
-    return [x[:, 128 * t : 128 * (t + 1)] for t in range(3)]
-
-
-def partners(g):
-    s = [swap8(t) for t in g]
-    lane = iota(g[0].shape, 1)
-    zero = jnp.zeros_like(g[0])
-    la = [g[1], g[0], jnp.where(lane < 16, s[2], zero)]
-    lb = [s[0], s[1], jnp.where((lane >= 16) & (lane < 32), s[2], zero)]
-    return la, lb, [s[1], s[0], zero]
+    s = jnp.where((lane & 8) == 0, pltpu.roll(x, 120, 1), pltpu.roll(x, 8, 1))
+    return jnp.where(lane < 112, s, 0.0)
+
+
+def swap_u(x):
+    lane = iota(x.shape, 1)
+    s = jnp.where(lane < 48, pltpu.roll(x, 80, 1), jnp.where(lane < 96, pltpu.roll(x, 48, 1), 0.0))
+    s = jnp.where((lane >= 112) & (lane < 115), pltpu.roll(x, 125, 1), s)
+    return jnp.where((lane >= 115) & (lane < 118), pltpu.roll(x, 3, 1), s)
+
+
+def signed(same, w):
+    return jnp.where(same, -w, w)
 
 
 GROUP = 4
@@ -115,9 +107,11 @@
     down_ref,
     feat_blk,
     feat_loc,
-    xy,
+    yu,
     sz,
     zz,
+    vb,
+    vv,
     xrows,
     gacc,
     gsend,
@@ -173,17 +167,19 @@
     lax.fori_loop(1, n_atom, greet_atom, 0)
 
     first = pl.ds(0, CHUNK)
-    xy[:, first] = jnp.zeros((XYR, CHUNK), BF16)
-    sz[:, first] = jnp.zeros((48, CHUNK), BF16)
+    yu[:, first] = jnp.zeros((LW, CHUNK), BF16)
+    sz[:, first] = jnp.zeros((SR, CHUNK), BF16)
     gacc[...] = jnp.zeros_like(gacc)
 
     sub = iota((8, CHUNK), 0)
     orders = (sub + 1).astype(F32)
+    third = jnp.where(sub < 3, sub, sub - 3)
+    x_orders = jnp.where(sub < 6, 3 * third + 3, 1).astype(F32)
     for copy in loads[:5]:
         copy.wait()
     mil_all[:, pl.ds(pl.multiple_of(ik * 128, 128), 128)] = jnp.concatenate(
         [miller_ref[...].astype(F32), jnp.zeros((5, 128), F32)], axis=0
-    )
+    ).astype(BF16)
     column = iota((NSPEC, 64), 1)
     tabs = [
         jnp.broadcast_to(
@@ -196,43 +192,58 @@
     def products(j):
         cols = pl.ds(pl.multiple_of(j * CHUNK, CHUNK), CHUNK)
         return lax.dot_general(
-            sz[:, cols], xy[:, cols], (((1,), (1,)), ((), ())), preferred_element_type=F32
-        )
+            sz[:, cols], yu[:, cols], (((1,), (1,)), ((), ())), preferred_element_type=F32
+        )
+
+    def row_of(i):
+        return jnp.broadcast_to(xrows[i : i + 1, :], (8, CHUNK))
+
+    def store(ref, r0, cols, upper, lower):
+        ref[r0 : r0 + 16, cols] = jnp.concatenate([upper, lower], axis=0).astype(BF16)
 
     def gather_chunk(j, _):
         part = products(jnp.maximum(j - 1, 0))
         cols = pl.ds(pl.multiple_of(j * CHUNK, CHUNK), CHUNK)
-        xc, xs = harmonics(jnp.broadcast_to(pos_ref[0:1, cols], (8, CHUNK)), orders)
+        xc, xs = harmonics(jnp.broadcast_to(pos_ref[0:1, cols], (8, CHUNK)), x_orders)
         xrows[0:8, :] = xc
         xrows[8:16, :] = xs
         yc, ys = harmonics(jnp.broadcast_to(pos_ref[1:2, cols], (8, CHUNK)), orders)
-        y16 = jnp.concatenate([yc, ys], axis=0).astype(BF16)
         zc, zs = harmonics(jnp.broadcast_to(pos_ref[2:3, cols], (8, CHUNK)), orders)
+        vc, vs = row_of(6), row_of(14)
+        ones = jnp.where(third == 1, vc, jnp.where(third == 2, vs, 1.0))
+        ones = jnp.where(sub < 6, ones, 0.0)
+        zero = jnp.zeros((8, CHUNK), F32)
         zz[0:8, cols] = zc
         zz[8:16, cols] = zs
-        z16 = jnp.concatenate([zc, zs], axis=0).astype(BF16)
-        for a in range(16):
-            xa = jnp.broadcast_to(xrows[a : a + 1, :], (8, CHUNK))
-            xy[16 * a : 16 * a + 16, cols] = jnp.concatenate([xa, xa], axis=0).astype(BF16) * y16
-        xy[256:272, cols] = jnp.concatenate([xc, xs], axis=0).astype(BF16)
-        xy[272:288, cols] = y16
-        one = jnp.where(sub == 0, 1.0, 0.0)
-        xy[288:304, cols] = jnp.concatenate([one, jnp.zeros_like(one)], axis=0).astype(BF16)
+        vb[0:8, cols] = vc
+        vb[8:16, cols] = vs
+        vv[:, cols] = ones
+        for i, r in enumerate((0, 1, 2, 11, 12, 13)):
+            u = row_of(r)
+            store(yu, 16 * i, cols, u * yc, u * ys)
+        store(yu, 96, cols, yc, ys)
+        store(
+            yu, 112, cols, jnp.where(sub < 3, xc, jnp.where(sub < 6, xs, jnp.where(sub == 6, 1.0, 0.0))), zero
+        )
         fb = feat_blk[:, cols].astype(F32)
         hot = jnp.broadcast_to(species_ref[0:1, cols], (8, CHUNK)) == sub
-        extra = jnp.zeros((8, CHUNK), F32)
+        sources = []
         for c in range(2):
             s = jnp.where(which[c], fb, 0.0) + jnp.where(hot, tabs[c], 0.0)
             s = jnp.broadcast_to(jnp.sum(s, axis=0, keepdims=True), (8, CHUNK))
-            extra = jnp.where(sub == c, s, extra)
-            sz[16 * c : 16 * c + 16, cols] = jnp.concatenate([s, s], axis=0).astype(BF16) * z16
-        sz[32:48, cols] = jnp.concatenate([extra, jnp.zeros_like(extra)], axis=0).astype(BF16)
-        gacc[:, 0:XYR] += part
+            s = s.astype(BF16).astype(F32)
+            sources.append(s)
+            szc, szs = s * zc, s * zs
+            store(sz, 48 * c, cols, szc, szs)
+            store(sz, 48 * c + 16, cols, szc * vc, szs * vc)
+            store(sz, 48 * c + 32, cols, szc * vs, szs * vs)
+        store(sz, 96, cols, jnp.where(sub < 3, sources[0], sources[1]) * ones, zero)
+        gacc[...] += part
         return 0
 
     lax.fori_loop(0, n_chunks, gather_chunk, 0)
-    gacc[:, 0:XYR] += products(n_chunks - 1)
-    gsend[...] = gacc[0:40, :].astype(BF16)
+    gacc[...] += products(n_chunks - 1)
+    gsend[...] = gacc[0:GR, :].astype(BF16)
 
     pl.semaphore_wait(barrier, n_ka - 1 + n_atom - 1)
 
@@ -281,56 +292,59 @@
         jnp.sum(jnp.where(column == 2 * ik + c, fw_ref[...], 0.0), axis=1, keepdims=True) * scaling
         for c in range(2)
     ]
-    signs, radials, radials0 = [], [], []
-    for t in range(3):
-        ta, p, tb, q, _ = lane_orders(t, (8, 128), 1)
-        signs.append((ta, tb))
-        pq = (p * p + q * q).astype(F32)
-        per_channel = []
-        for mag in (jnp.sqrt(pq + r8 * r8), jnp.sqrt(pq)):
-            acc = [jnp.zeros((8, 128), F32) for _ in range(2)]
-            for b in range(NRBF):
-                z = (mag - b * (K_CUTOFF / (NRBF - 1))) * (NRBF / K_CUTOFF)
-                e = jnp.exp(-(z * z))
-                for c in range(2):
-                    acc[c] = acc[c] + weights[c][b : b + 1, :] * e
-            per_channel.append(acc)
-        radials.append(per_channel[0])
-        radials0.append(jnp.where(sub1 == 0, per_channel[1][0], per_channel[1][1]))
-
-    expand = []
-    row = iota((96, 128), 0)
-    for t in range(3):
-        _, p, _, q, used = lane_orders(t, (96, 128), 1)
-        expand.append(jnp.where(used & (row == p * 9 + q), 1.0, 0.0))
-    expand = jnp.concatenate(expand, axis=1).astype(BF16)
+    tu, a, ty, q, _ = lane_orders((8, 128), 1)
+    af, qq = a.astype(F32) * 3.0, (q * q).astype(F32)
+    third1 = jnp.where(sub1 < 3, sub1, sub1 - 3)
+    b_row = jnp.where((third1 > 0) & (sub1 < 6), 1.0, 0.0)
+    tv_row = jnp.where(third1 == 2, 1, 0)
+
+    def radial_of(m, r):
+        mag = jnp.sqrt(m * m + qq + r * r)
+        acc = [jnp.zeros((8, 128), F32) for _ in range(2)]
+        for b in range(NRBF):
+            z = (mag - b * (K_CUTOFF / (NRBF - 1))) * (NRBF / K_CUTOFF)
+            e = jnp.exp(-(z * z))
+            for c in range(2):
+                acc[c] = acc[c] + weights[c][b : b + 1, :] * e
+        return acc
+
+    zero1 = jnp.zeros((8, 128), F32)
+    rad_0 = radial_of(af, r8)
+    rad_p, rad_m = radial_of(af + 1.0, r8), radial_of(af - 1.0, r8)
+    single_p, single_m = [
+        jnp.where(sub1 < 3, v[0], v[1]) for v in (radial_of(af + b_row, zero1), radial_of(af - b_row, zero1))
+    ]
 
     mil_copy(mil_all.at[:, 0 : n_vec - 128], mil_all.at[:, 0 : n_vec - 128], ik).wait_recv()
-    codes = iota((96, CHUNK), 0).astype(F32)
-    counts = jnp.zeros((48, 96), F32)
+    _, a_r, _, q_r, used = lane_orders((LW, CHUNK), 0)
+    codes = jnp.where(used, a_r * 9 + q_r, -1).astype(F32)
+    b_sub = jnp.where(third == 0, 0.0, 1.0)
+    b_sub = jnp.where(sub < 6, b_sub, -1.0)
+    counts = jnp.zeros((128, LW), F32)
     for j in range(n_vec // CHUNK):
-        m = mil_all[:, CHUNK * j : CHUNK * (j + 1)]
+        m = mil_all[:, CHUNK * j : CHUNK * (j + 1)].astype(F32)
         mx, my, mz = [jnp.broadcast_to(m[i : i + 1, :], (8, CHUNK)) for i in range(3)]
-        gx, gy, gz = [jnp.where(v < 0, -1.0, 1.0) for v in (mx, my, mz)]
-        code = jnp.abs(mx) * 9.0 + jnp.abs(my)
-        hot_xy = jnp.where(codes == jnp.broadcast_to(code[0:1, :], (96, CHUNK)), 1.0, 0.0).astype(BF16)
-        az = jnp.abs(mz)
+        ma = jnp.round(mx * (1.0 / 3.0))
+        mb = mx - 3.0 * ma
+        ga, gb, gy, gz = [jnp.where(v < 0, -1.0, 1.0) for v in (ma, mb, my, mz)]
+        code = jnp.abs(ma) * 9.0 + jnp.abs(my)
+        hot_uy = jnp.where(codes == jnp.broadcast_to(code[0:1, :], (LW, CHUNK)), 1.0, 0.0).astype(BF16)
+        ab, ar, br, aq, bq, qr = ga * gb, ga * gz, gb * gz, ga * gy, gb * gy, gy * gz
+        az, absb = jnp.abs(mz), jnp.abs(mb)
         hz = jnp.where(az == orders, 1.0, 0.0)
-        h0 = jnp.where((az == 0.0) & (sub < 2), 1.0, 0.0)
+        h1 = hz * absb
+        h0 = hz - h1
+        hs = jnp.where((az == 0.0) & (absb == b_sub), 1.0, 0.0)
         wr = jnp.concatenate(
-            [hz, hz * (gy * gz), hz * (gx * gz), hz * (gx * gy), h0, h0 * (gx * gy)], axis=0
+            [h1, h1 * ab, h1 * ar, h1 * br, h1 * aq, h1 * bq, h1 * qr, h1 * (ab * qr)]
+            + [h0, h0 * aq, h0 * ar, h0 * qr]
+            + [hs, hs * ab, hs * aq, hs * bq],
+            axis=0,
         ).astype(BF16)
         counts = counts + lax.dot_general(
-            wr, hot_xy, (((1,), (1,)), ((), ())), preferred_element_type=F32
-        )
-    high = jnp.floor(counts * (1.0 / 256.0))
-    low = counts - 256.0 * high
-    wt = 256.0 * jnp.dot(high.astype(BF16), expand, preferred_element_type=F32) + jnp.dot(
-        low.astype(BF16), expand, preferred_element_type=F32
-    )
-    w_plain, w_yz, w_xz, w_xy, w_plain0, w_xy0 = [
-        tiles_of(wt[8 * i : 8 * i + 8, :]) for i in range(6)
-    ]
+            wr, hot_uy, (((1,), (1,)), ((), ())), preferred_element_type=F32
+        )
+    w = [counts[8 * i : 8 * i + 8, :] for i in range(16)]
 
     pltpu.make_async_remote_copy(
         src_ref=grecv.at[0 : n_atom - 1],
@@ -345,30 +359,42 @@
     for i in range(1, n_atom):
         g = g + grecv[i].astype(F32)
 
+    def mixed(plus, minus, plain, crossed):
+        half_s, half_d = 0.5 * (plus + minus), 0.5 * (plus - minus)
+        return half_s * plain + half_d * crossed, half_s * crossed + half_d * plain
+
+    same_uy = tu == ty
     rows = []
     for c in range(2):
-        gz = [tiles_of(g[16 * c + 8 * tz : 16 * c + 8 * tz + 8, :]) for tz in range(2)]
-        swapped = [partners(v) for v in gz]
-        for tz in range(2):
-            la, lb, _ = swapped[1 - tz]
-            _, _, lab = swapped[tz]
-            out = []
-            for t in range(3):
-                ta, tb = signs[t]
-                u = jnp.where(tb == tz, -lb[t], lb[t]) * w_yz[t]
-                v = jnp.where(ta == tz, -la[t], la[t]) * w_xz[t]
-                w = jnp.where(ta == tb, -lab[t], lab[t]) * w_xy[t]
-                out.append((gz[tz][t] * w_plain[t] + u + v + w) * radials[t][c])
-            rows.append(jnp.concatenate(out, axis=1))
-    g0 = tiles_of(g[32:40, :])
-    _, _, lab = partners(g0)
-    out = []
-    for t in range(3):
-        ta, tb = signs[t]
-        w = jnp.where(ta == tb, -lab[t], lab[t]) * w_xy0[t]
-        out.append((g0[t] * w_plain0[t] + w) * radials0[t])
-    rows.append(jnp.concatenate(out, axis=1))
-    rows.append(jnp.zeros((8, LW), F32))
+        gb = [[g[48 * c + 16 * v + 8 * t : 48 * c + 16 * v + 8 * t + 8, :] for t in range(2)] for v in range(3)]
+        gu = [[swap_u(x) for x in pair] for pair in gb]
+        gy = [[swap_y(x) for x in pair] for pair in gb]
+        guy = [[swap_u(x) for x in pair] for pair in gy]
+        for t in range(2):
+            h = w[8] * gb[0][t] + signed(same_uy, w[9]) * guy[0][t]
+            h = h + signed(tu == t, w[10]) * gu[0][1 - t] + signed(ty == t, w[11]) * gy[0][1 - t]
+            rows.append(h * rad_0[c])
+        c_0, c_ab = mixed(rad_p[c], rad_m[c], w[0], w[1])
+        c_ar, c_br = mixed(rad_p[c], rad_m[c], w[2], w[3])
+        c_aq, c_bq = mixed(rad_p[c], rad_m[c], w[4], w[5])
+        c_qr, c_all = mixed(rad_p[c], rad_m[c], w[6], w[7])
+        for v in (1, 2):
+            tv, o = v - 1, 3 - v
+            for t in range(2):
+                h = c_0 * gb[v][t] + signed(same_uy, c_aq) * guy[v][t]
+                h = h + signed(tu == t, c_ar) * gu[v][1 - t] + signed(ty == t, c_qr) * gy[v][1 - t]
+                h = h + signed(tu == tv, c_ab) * gu[o][t] + signed(ty == tv, c_bq) * gy[o][t]
+                h = h + (-c_br if tv == t else c_br) * gb[o][1 - t]
+                odd = same_uy if (tv + t) % 2 == 1 else tu != ty
+                rows.append(h + signed(odd, c_all) * guy[o][1 - t])
+    g0 = g[96:104, :]
+    over = jnp.where(third1 == 1, pltpu.roll(g0, 7, 0), pltpu.roll(g0, 1, 0))
+    over = jnp.where(b_row > 0.0, over, 0.0)
+    c_0, c_ab = mixed(single_p, single_m, w[12], w[13])
+    c_aq, c_bq = mixed(single_p, single_m, w[14], w[15])
+    h = c_0 * g0 + signed(same_uy, c_aq) * swap_u(swap_y(g0))
+    h = h + signed(tu == tv_row, c_ab) * swap_u(over) + signed(ty == tv_row, c_bq) * swap_y(over)
+    rows += [h, jnp.zeros((8, LW), F32)]
     hmat[...] = jnp.concatenate(rows, axis=0).astype(BF16)
 
     def m_copy(slot, to):
@@ -383,10 +409,15 @@
 
     def message_of(d, cols):
         zc, zs = zz[0:8, cols], zz[8:16, cols]
+        vs = (None, vb[0:8, cols], vb[8:16, cols])
+        single = d[96:104, :] * vv[:, cols]
         parts = []
         for c in range(2):
-            s = d[16 * c : 16 * c + 8, :] * zc + d[16 * c + 8 : 16 * c + 16, :] * zs
-            s = s + jnp.where(sub == c, d[32:40, :], 0.0)
+            s = jnp.where((sub < 3) == (c == 0), single, 0.0)
+            for v in range(3):
+                r = 48 * c + 16 * v
+                e = d[r : r + 8, :] * zc + d[r + 8 : r + 16, :] * zs
+                s = s + (e if v == 0 else e * vs[v])
             s = jnp.sum(s, axis=0, keepdims=True)
             parts += [s[:, 128 * i : 128 * (i + 1)] for i in range(CHUNK // 128)]
         return jnp.concatenate(parts, axis=0).astype(BF16)
@@ -394,7 +425,7 @@
     def send_messages(i, _):
         to = [partner(GROUP * i + k) for k in range(GROUP)]
         cols = [pl.ds(pl.multiple_of(j * CHUNK, CHUNK), CHUNK) for j in to]
-        ds = [jnp.dot(hmat[:, 0:XYR], xy[:, c], preferred_element_type=F32) for c in cols]
+        ds = [jnp.dot(hmat[...], yu[:, c], preferred_element_type=F32) for c in cols]
         for k in range(GROUP):
             msgs[to[k]] = message_of(ds[k], cols[k])
         for k in range(GROUP):
@@ -470,15 +501,17 @@
                 pltpu.VMEM((channels, hid), BF16),
                 pltpu.VMEM((8, atoms), BF16),
                 pltpu.VMEM((channels, local), BF16),
-                pltpu.VMEM((XYR, atoms), BF16),
-                pltpu.VMEM((48, atoms), BF16),
+                pltpu.VMEM((LW, atoms), BF16),
+                pltpu.VMEM((SR, atoms), BF16),
                 pltpu.VMEM((16, atoms), F32),
+                pltpu.VMEM((16, atoms), F32),
+                pltpu.VMEM((8, atoms), F32),
                 pltpu.VMEM((16, CHUNK), F32),
-                pltpu.VMEM((48, LW), F32),
-                pltpu.VMEM((40, LW), BF16),
-                pltpu.VMEM((n_atom, 40, LW), BF16),
-                pltpu.VMEM((8, n_vectors), F32),
-                pltpu.VMEM((48, LW), BF16),
+                pltpu.VMEM((SR, LW), F32),
+                pltpu.VMEM((GR, LW), BF16),
+                pltpu.VMEM((n_atom, GR, LW), BF16),
+                pltpu.VMEM((8, n_vectors), BF16),
+                pltpu.VMEM((SR, LW), BF16),
                 pltpu.VMEM((n_ka, 8, 128), BF16),
                 pltpu.VMEM((n_ka, 8, 128), BF16),
                 pltpu.VMEM((n_ka * 8, 128), F32),

time: 30.9 us -> 31 us (level)
  no operation moved by 1% of the time
where the time goes in v4:
time: 31 us; the launch traced here: 30.9 us
  Pallas kernels  30.3 us (98%)
  local copies, waits for them, and re-layouts  0.63 us (2%)
    pallas_call x1, Pallas kernels, body(): pl.pallas_call(functools.partial(body_kernel, (n_atom, n_ka, ny, nz, atom...  30.3 us
    unnamed x1, local copies, waits for them, and re-layouts  0.63 us

profile of v4, /device:TPU:1, one launch (start us, length us, event | category | flops | bytes accessed | tf_op | source)
XLA Modules:
  0.0 30.9 jit_solution(2451055794015859097)
XLA Ops:
  0.0 30.3 %ewald.1 = bf16[64,512]{1,0:T(8,128)(2,1)S(1)} custom-call(f32[3,16384]{1,0:T(4,128)} %pos_hbm.1, bf16[64,16384]{1,0:T(8,128)(2,1)} %feat_hbm.1, s32[1,16384]{1,0:T(1,128)} %bitcast.5, s32[3,128]{1,0:T(4,128)} %miller_hbm.1, f32[8,64]{1,0:T(8,128)} %bitcast.8, f32[16,64]{1,0:T(8,128)} %bitcast.7, f32[1,64]{1,0:T(1,128)} %bitcast.9, bf16[64,256]{1,0:T(8,128)(2,1)} %bitcast.6, ...), custom_call_target="tpu_custom_call" | custom-call | tf_op jit(solution)/shard_map/ewald/pallas_call | solution.py:488
  30.3 0.6 %copy.11 = bf16[64,512]{1,0:T(8,128)(2,1)} copy(bf16[64,512]{1,0:T(8,128)(2,1)S(1)} %ewald.1) | data formatting | bytes 131072

commit v5 on v4

--- a/solution.py
+++ b/solution.py
@@ -17,6 +17,7 @@
 SR = 112
 GR = 104
 CHUNK = 512
+DEPTH = 4096
 K_CUTOFF = 14.0
 
 def _fit():
@@ -137,8 +138,20 @@
 
     barrier = pltpu.get_barrier_semaphore()
 
-    def greet_ka(d, _):
-        pl.semaphore_signal(barrier, inc=1, device_id=(ia, lax.rem(ik + d, n_ka)), device_id_type=MESH)
+    iy, iz = ik // nz, lax.rem(ik, nz)
+
+    def along_y(d):
+        return lax.rem(iy + d, ny) * nz + iz
+
+    def along_z(d):
+        return iy * nz + lax.rem(iz + d, nz)
+
+    def greet_z(d, _):
+        pl.semaphore_signal(barrier, inc=1, device_id=(ia, along_z(d)), device_id_type=MESH)
+        return 0
+
+    def greet_y(d, _):
+        pl.semaphore_signal(barrier, inc=1, device_id=(ia, along_y(d)), device_id_type=MESH)
         return 0
 
     def greet_atom(d, _):
@@ -163,14 +176,11 @@
         copy = pltpu.make_async_copy(src, dst, local_sem.at[i])
         copy.start()
         loads.append(copy)
-    lax.fori_loop(1, n_ka, greet_ka, 0)
+    lax.fori_loop(1, nz, greet_z, 0)
+    lax.fori_loop(1, ny, greet_y, 0)
     lax.fori_loop(1, n_atom, greet_atom, 0)
 
-    first = pl.ds(0, CHUNK)
-    yu[:, first] = jnp.zeros((LW, CHUNK), BF16)
-    sz[:, first] = jnp.zeros((SR, CHUNK), BF16)
     gacc[...] = jnp.zeros_like(gacc)
-
     sub = iota((8, CHUNK), 0)
     orders = (sub + 1).astype(F32)
     third = jnp.where(sub < 3, sub, sub - 3)
@@ -189,12 +199,6 @@
     ]
     which = [sub == lax.rem(2 * ik, 8) + c for c in range(2)]
 
-    def products(j):
-        cols = pl.ds(pl.multiple_of(j * CHUNK, CHUNK), CHUNK)
-        return lax.dot_general(
-            sz[:, cols], yu[:, cols], (((1,), (1,)), ((), ())), preferred_element_type=F32
-        )
-
     def row_of(i):
         return jnp.broadcast_to(xrows[i : i + 1, :], (8, CHUNK))
 
@@ -202,7 +206,6 @@
         ref[r0 : r0 + 16, cols] = jnp.concatenate([upper, lower], axis=0).astype(BF16)
 
     def gather_chunk(j, _):
-        part = products(jnp.maximum(j - 1, 0))
         cols = pl.ds(pl.multiple_of(j * CHUNK, CHUNK), CHUNK)
         xc, xs = harmonics(jnp.broadcast_to(pos_ref[0:1, cols], (8, CHUNK)), x_orders)
         xrows[0:8, :] = xc
@@ -238,14 +241,21 @@
             store(sz, 48 * c + 16, cols, szc * vc, szs * vc)
             store(sz, 48 * c + 32, cols, szc * vs, szs * vs)
         store(sz, 96, cols, jnp.where(sub < 3, sources[0], sources[1]) * ones, zero)
-        gacc[...] += part
         return 0
 
     lax.fori_loop(0, n_chunks, gather_chunk, 0)
-    gacc[...] += products(n_chunks - 1)
+
+    def add_products(j, _):
+        cols = pl.ds(pl.multiple_of(j * DEPTH, DEPTH), DEPTH)
+        gacc[...] += lax.dot_general(
+            sz[:, cols], yu[:, cols], (((1,), (1,)), ((), ())), preferred_element_type=F32
+        )
+        return 0
+
+    lax.fori_loop(0, atoms // DEPTH, add_products, 0)
     gsend[...] = gacc[0:GR, :].astype(BF16)
 
-    pl.semaphore_wait(barrier, n_ka - 1 + n_atom - 1)
+    pl.semaphore_wait(barrier, nz - 1 + ny - 1 + n_atom - 1)
 
     def g_copy(slot, to):
         return pltpu.make_async_remote_copy(
@@ -261,12 +271,20 @@
         g_copy(ia, lax.rem(ia + d, n_atom)).start()
         return 0
 
-    def mil_copy(ref, dst, to):
+    def mil_copy(ref, to, stage):
         return pltpu.make_async_remote_copy(
-            src_ref=ref, dst_ref=dst, send_sem=mil_send, recv_sem=mil_recv, device_id=(ia, to), device_id_type=MESH
+            src_ref=ref,
+            dst_ref=ref,
+            send_sem=mil_send.at[stage],
+            recv_sem=mil_recv.at[stage],
+            device_id=(ia, to),
+            device_id_type=MESH,
         )
 
     own = mil_all.at[:, pl.ds(pl.multiple_of(ik * 128, 128), 128)]
+    own_row = mil_all.at[:, pl.ds(pl.multiple_of(iy * (nz * 128), nz * 128), nz * 128)]
+    all_z = mil_copy(mil_all.at[:, 0 : (nz - 1) * 128], ik, 0)
+    all_y = mil_copy(mil_all.at[:, 0 : (ny - 1) * nz * 128], ik, 1)
 
     def farther(k, n):
         return n // 2 + (1 - 2 * lax.rem(k, 2)) * ((k + 1) // 2)
@@ -276,11 +294,15 @@
         y, z = lax.rem(ik // nz + dy, ny), lax.rem(lax.rem(ik, nz) + dz, nz)
         return y * nz + z
 
-    def send_miller(i, _):
-        mil_copy(own, own, partner(i)).start()
-        return 0
-
-    lax.fori_loop(0, n_ka - 1, send_miller, 0)
+    def send_z(i, _):
+        mil_copy(own, along_z(farther(i, nz)), 0).start()
+        return 0
+
+    def send_y(d, _):
+        mil_copy(own_row, along_y(d), 1).start()
+        return 0
+
+    lax.fori_loop(0, nz - 1, send_z, 0)
     lax.fori_loop(1, n_atom, send_g, 0)
 
     for copy in loads[5:]:
@@ -315,7 +337,23 @@
         jnp.where(sub1 < 3, v[0], v[1]) for v in (radial_of(af + b_row, zero1), radial_of(af - b_row, zero1))
     ]
 
-    mil_copy(mil_all.at[:, 0 : n_vec - 128], mil_all.at[:, 0 : n_vec - 128], ik).wait_recv()
+    all_z.wait_recv()
+    lax.fori_loop(1, ny, send_y, 0)
+
+    pltpu.make_async_remote_copy(
+        src_ref=grecv.at[0 : n_atom - 1],
+        dst_ref=grecv.at[0 : n_atom - 1],
+        send_sem=g_send,
+        recv_sem=g_recv,
+        device_id=(ia, ik),
+        device_id_type=MESH,
+    ).wait_recv()
+    grecv[ia] = gsend[...]
+    g = grecv[0].astype(F32)
+    for i in range(1, n_atom):
+        g = g + grecv[i].astype(F32)
+
+    all_y.wait_recv()
     _, a_r, _, q_r, used = lane_orders((LW, CHUNK), 0)
     codes = jnp.where(used, a_r * 9 + q_r, -1).astype(F32)
     b_sub = jnp.where(third == 0, 0.0, 1.0)
@@ -345,19 +383,6 @@
             wr, hot_uy, (((1,), (1,)), ((), ())), preferred_element_type=F32
         )
     w = [counts[8 * i : 8 * i + 8, :] for i in range(16)]
-
-    pltpu.make_async_remote_copy(
-        src_ref=grecv.at[0 : n_atom - 1],
-        dst_ref=grecv.at[0 : n_atom - 1],
-        send_sem=g_send,
-        recv_sem=g_recv,
-        device_id=(ia, ik),
-        device_id_type=MESH,
-    ).wait_recv()
-    grecv[ia] = gsend[...]
-    g = grecv[0].astype(F32)
-    for i in range(1, n_atom):
-        g = g + grecv[i].astype(F32)
 
     def mixed(plus, minus, plain, crossed):
         half_s, half_d = 0.5 * (plus + minus), 0.5 * (plus - minus)
@@ -462,7 +487,8 @@
     update = jnp.dot(down_ref[...], hidden, preferred_element_type=F32)
     out_ref[...] = (feat_loc[...].astype(F32) + update).astype(BF16)
 
-    mil_copy(mil_all.at[:, 0 : n_vec - 128], mil_all.at[:, 0 : n_vec - 128], ik).wait_send()
+    all_z.wait_send()
+    all_y.wait_send()
     all_messages().wait_send()
     pltpu.make_async_remote_copy(
         src_ref=grecv.at[0 : n_atom - 1],
@@ -516,8 +542,8 @@
                 pltpu.VMEM((n_ka, 8, 128), BF16),
                 pltpu.VMEM((n_ka * 8, 128), F32),
                 pltpu.SemaphoreType.DMA((10,)),
-                pltpu.SemaphoreType.DMA,
-                pltpu.SemaphoreType.DMA,
+                pltpu.SemaphoreType.DMA((2,)),
+                pltpu.SemaphoreType.DMA((2,)),
                 pltpu.SemaphoreType.DMA,
                 pltpu.SemaphoreType.DMA,
                 pltpu.SemaphoreType.DMA,

time: 31 us -> 27.1 us (0.87)
  the two profiles are of different devices: /device:TPU:1 before, /device:TPU:2 now
where the time goes in v5:
time: 27.1 us
  Pallas kernels  26.4 us (97%)
  local copies, waits for them, and re-layouts  0.63 us (2%)
    pallas_call x1, Pallas kernels, body(): pl.pallas_call(functools.partial(body_kernel, (n_atom, n_ka, ny, nz, atom...  26.4 us
    unnamed x1, local copies, waits for them, and re-layouts  0.63 us

profile of v5, /device:TPU:2, one launch (start us, length us, event | category | flops | bytes accessed | tf_op | source)
XLA Modules:
  0.0 27.1 jit_solution(6638609253552068331)
XLA Ops:
  0.0 26.4 %ewald.1 = bf16[64,512]{1,0:T(8,128)(2,1)S(1)} custom-call(f32[3,16384]{1,0:T(4,128)} %pos_hbm.1, bf16[64,16384]{1,0:T(8,128)(2,1)} %feat_hbm.1, s32[1,16384]{1,0:T(1,128)} %bitcast.5, s32[3,128]{1,0:T(4,128)} %miller_hbm.1, f32[8,64]{1,0:T(8,128)} %bitcast.8, f32[16,64]{1,0:T(8,128)} %bitcast.7, f32[1,64]{1,0:T(1,128)} %bitcast.9, bf16[64,256]{1,0:T(8,128)(2,1)} %bitcast.6, ...), custom_call_target="tpu_custom_call" | custom-call | tf_op jit(solution)/shard_map/ewald/pallas_call | solution.py:514
  26.4 0.6 %copy.11 = bf16[64,512]{1,0:T(8,128)(2,1)} copy(bf16[64,512]{1,0:T(8,128)(2,1)S(1)} %ewald.1) | data formatting | bytes 131072

commit v6 on v5

--- a/solution.py
+++ b/solution.py
@@ -17,7 +17,8 @@
 SR = 112
 GR = 104
 CHUNK = 512
-DEPTH = 4096
+DEPTH = 8192
+EARLY = 14
 K_CUTOFF = 14.0
 
 def _fit():
@@ -243,34 +244,6 @@
         store(sz, 96, cols, jnp.where(sub < 3, sources[0], sources[1]) * ones, zero)
         return 0
 
-    lax.fori_loop(0, n_chunks, gather_chunk, 0)
-
-    def add_products(j, _):
-        cols = pl.ds(pl.multiple_of(j * DEPTH, DEPTH), DEPTH)
-        gacc[...] += lax.dot_general(
-            sz[:, cols], yu[:, cols], (((1,), (1,)), ((), ())), preferred_element_type=F32
-        )
-        return 0
-
-    lax.fori_loop(0, atoms // DEPTH, add_products, 0)
-    gsend[...] = gacc[0:GR, :].astype(BF16)
-
-    pl.semaphore_wait(barrier, nz - 1 + ny - 1 + n_atom - 1)
-
-    def g_copy(slot, to):
-        return pltpu.make_async_remote_copy(
-            src_ref=gsend,
-            dst_ref=grecv.at[slot],
-            send_sem=g_send,
-            recv_sem=g_recv,
-            device_id=(to, ik),
-            device_id_type=MESH,
-        )
-
-    def send_g(d, _):
-        g_copy(ia, lax.rem(ia + d, n_atom)).start()
-        return 0
-
     def mil_copy(ref, to, stage):
         return pltpu.make_async_remote_copy(
             src_ref=ref,
@@ -302,8 +275,53 @@
         mil_copy(own_row, along_y(d), 1).start()
         return 0
 
+    lax.fori_loop(0, EARLY, gather_chunk, 0)
+    pl.semaphore_wait(barrier, nz - 1 + ny - 1 + n_atom - 1)
     lax.fori_loop(0, nz - 1, send_z, 0)
-    lax.fori_loop(1, n_atom, send_g, 0)
+    lax.fori_loop(EARLY, n_chunks, gather_chunk, 0)
+
+    halves = ((0, SR, GR),)
+
+    def g_copy(half, slot, to):
+        lo, _, hi = halves[half]
+        return pltpu.make_async_remote_copy(
+            src_ref=gsend.at[lo:hi],
+            dst_ref=grecv.at[slot, lo:hi],
+            send_sem=g_send.at[half],
+            recv_sem=g_recv.at[half],
+            device_id=(to, ik),
+            device_id_type=MESH,
+        )
+
+    def all_g(half):
+        lo, _, hi = halves[half]
+        part = grecv.at[0 : n_atom - 1, lo:hi]
+        return pltpu.make_async_remote_copy(
+            src_ref=part,
+            dst_ref=part,
+            send_sem=g_send.at[half],
+            recv_sem=g_recv.at[half],
+            device_id=(ia, ik),
+            device_id_type=MESH,
+        )
+
+    for half, (lo, up_to, hi) in enumerate(halves):
+
+        def add_products(j, _, lo=lo, up_to=up_to):
+            cols = pl.ds(pl.multiple_of(j * DEPTH, DEPTH), DEPTH)
+            gacc[lo:up_to, :] += lax.dot_general(
+                sz[lo:up_to, cols], yu[:, cols], (((1,), (1,)), ((), ())), preferred_element_type=F32
+            )
+            return 0
+
+        lax.fori_loop(0, atoms // DEPTH, add_products, 0)
+        gsend[lo:hi, :] = gacc[lo:hi, :].astype(BF16)
+
+        def send_g(i, _, half=half):
+            g_copy(half, ia, lax.rem(ia + 1 + lax.rem(i + 2, n_atom - 1), n_atom)).start()
+            return 0
+
+        lax.fori_loop(0, n_atom - 1, send_g, 0)
 
     for copy in loads[5:]:
         copy.wait()
@@ -339,19 +357,6 @@
 
     all_z.wait_recv()
     lax.fori_loop(1, ny, send_y, 0)
-
-    pltpu.make_async_remote_copy(
-        src_ref=grecv.at[0 : n_atom - 1],
-        dst_ref=grecv.at[0 : n_atom - 1],
-        send_sem=g_send,
-        recv_sem=g_recv,
-        device_id=(ia, ik),
-        device_id_type=MESH,
-    ).wait_recv()
-    grecv[ia] = gsend[...]
-    g = grecv[0].astype(F32)
-    for i in range(1, n_atom):
-        g = g + grecv[i].astype(F32)
 
     all_y.wait_recv()
     _, a_r, _, q_r, used = lane_orders((LW, CHUNK), 0)
@@ -383,6 +388,12 @@
             wr, hot_uy, (((1,), (1,)), ((), ())), preferred_element_type=F32
         )
     w = [counts[8 * i : 8 * i + 8, :] for i in range(16)]
+
+    all_g(0).wait_recv()
+    grecv[ia] = gsend[...]
+    g = grecv[0].astype(F32)
+    for i in range(1, n_atom):
+        g = g + grecv[i].astype(F32)
 
     def mixed(plus, minus, plain, crossed):
         half_s, half_d = 0.5 * (plus + minus), 0.5 * (plus - minus)
@@ -453,7 +464,7 @@
         ds = [jnp.dot(hmat[...], yu[:, c], preferred_element_type=F32) for c in cols]
         for k in range(GROUP):
             msgs[to[k]] = message_of(ds[k], cols[k])
-        for k in range(GROUP):
+
             @pl.when(to[k] != ik)
             def _():
                 m_copy(ik, to[k]).start()
@@ -490,14 +501,7 @@
     all_z.wait_send()
     all_y.wait_send()
     all_messages().wait_send()
-    pltpu.make_async_remote_copy(
-        src_ref=grecv.at[0 : n_atom - 1],
-        dst_ref=grecv.at[0 : n_atom - 1],
-        send_sem=g_send,
-        recv_sem=g_recv,
-        device_id=(ia, ik),
-        device_id_type=MESH,
-    ).wait_send()
+    all_g(0).wait_send()
 
 
 def solution(mesh):
@@ -544,8 +548,8 @@
                 pltpu.SemaphoreType.DMA((10,)),
                 pltpu.SemaphoreType.DMA((2,)),
                 pltpu.SemaphoreType.DMA((2,)),
-                pltpu.SemaphoreType.DMA,
-                pltpu.SemaphoreType.DMA,
+                pltpu.SemaphoreType.DMA((1,)),
+                pltpu.SemaphoreType.DMA((1,)),
                 pltpu.SemaphoreType.DMA,
                 pltpu.SemaphoreType.DMA,
             ],

time: 27.1 us -> 25 us (0.923)
  the two profiles are of different devices: /device:TPU:2 before, /device:TPU:1 now
where the time goes in v6:
time: 25 us; the launch traced here: 24.9 us
  Pallas kernels  24.3 us (97%)
  local copies, waits for them, and re-layouts  0.63 us (3%)
    pallas_call x1, Pallas kernels, body(): pl.pallas_call(functools.partial(body_kernel, (n_atom, n_ka, ny, nz, atom...  24.3 us
    unnamed x1, local copies, waits for them, and re-layouts  0.63 us

profile of v6, /device:TPU:1, one launch (start us, length us, event | category | flops | bytes accessed | tf_op | source)
XLA Modules:
  0.0 24.9 jit_solution(16797354618442290168)
XLA Ops:
  0.0 24.3 %ewald.1 = bf16[64,512]{1,0:T(8,128)(2,1)S(1)} custom-call(f32[3,16384]{1,0:T(4,128)} %pos_hbm.1, bf16[64,16384]{1,0:T(8,128)(2,1)} %feat_hbm.1, s32[1,16384]{1,0:T(1,128)} %bitcast.5, s32[3,128]{1,0:T(4,128)} %miller_hbm.1, f32[8,64]{1,0:T(8,128)} %bitcast.8, f32[16,64]{1,0:T(8,128)} %bitcast.7, f32[1,64]{1,0:T(1,128)} %bitcast.9, bf16[64,256]{1,0:T(8,128)(2,1)} %bitcast.6, ...), custom_call_target="tpu_custom_call" | custom-call | tf_op jit(solution)/shard_map/ewald/pallas_call | solution.py:518
  24.3 0.6 %copy.11 = bf16[64,512]{1,0:T(8,128)(2,1)} copy(bf16[64,512]{1,0:T(8,128)(2,1)S(1)} %ewald.1) | data formatting | bytes 131072

commit v7 on v6

--- a/solution.py
+++ b/solution.py
@@ -17,8 +17,7 @@
 SR = 112
 GR = 104
 CHUNK = 512
-DEPTH = 8192
-EARLY = 14
+EARLY = 6
 K_CUTOFF = 14.0
 
 def _fit():
@@ -85,6 +84,7 @@
 
 
 GROUP = 4
+PAD = 128
 
 
 def body_kernel(
@@ -115,7 +115,9 @@
     vb,
     vv,
     xrows,
-    gacc,
+    counts_ref,
+    up_pad,
+    hmat_b,
     gsend,
     grecv,
     mil_all,
@@ -181,7 +183,9 @@
     lax.fori_loop(1, ny, greet_y, 0)
     lax.fori_loop(1, n_atom, greet_atom, 0)
 
-    gacc[...] = jnp.zeros_like(gacc)
+    first = pl.ds(0, 2 * CHUNK)
+    yu[:, first] = jnp.zeros((LW, 2 * CHUNK), BF16)
+    sz[:, first] = jnp.zeros((SR, 2 * CHUNK), BF16)
     sub = iota((8, CHUNK), 0)
     orders = (sub + 1).astype(F32)
     third = jnp.where(sub < 3, sub, sub - 3)
@@ -206,6 +210,26 @@
     def store(ref, r0, cols, upper, lower):
         ref[r0 : r0 + 16, cols] = jnp.concatenate([upper, lower], axis=0).astype(BF16)
 
+    def twice(x):
+        return jnp.concatenate([x, x], axis=0).astype(BF16)
+
+    def tile(ref, j):
+        return ref[:, pl.ds(pl.multiple_of(j * 256, 256), 256)]
+
+    def multiply(accs, j):
+        for i in range(2):
+            pltpu.matmul_push_rhs(
+                jnp.concatenate([tile(yu, 4 * j + 2 * i), tile(yu, 4 * j + 2 * i + 1)], axis=0), 0, i, transpose=True
+            )
+            pltpu.matmul_acc_lhs(accs[2 * i], tile(sz, 4 * j + 2 * i), load_staged_rhs=0)
+            pltpu.matmul_acc_lhs(accs[2 * i + 1], tile(sz, 4 * j + 2 * i + 1))
+
+    def diagonal(accs):
+        total = 0.0
+        for i, acc in enumerate(accs):
+            total = total + pltpu.matmul_pop(acc)[:, LW * (i % 2) : LW * (i % 2) + LW]
+        return total
+
     def gather_chunk(j, _):
         cols = pl.ds(pl.multiple_of(j * CHUNK, CHUNK), CHUNK)
         xc, xs = harmonics(jnp.broadcast_to(pos_ref[0:1, cols], (8, CHUNK)), x_orders)
@@ -217,6 +241,7 @@
         ones = jnp.where(third == 1, vc, jnp.where(third == 2, vs, 1.0))
         ones = jnp.where(sub < 6, ones, 0.0)
         zero = jnp.zeros((8, CHUNK), F32)
+        y16 = jnp.concatenate([yc, ys], axis=0).astype(BF16)
         zz[0:8, cols] = zc
         zz[8:16, cols] = zs
         vb[0:8, cols] = vc
@@ -224,23 +249,25 @@
         vv[:, cols] = ones
         for i, r in enumerate((0, 1, 2, 11, 12, 13)):
             u = row_of(r)
-            store(yu, 16 * i, cols, u * yc, u * ys)
-        store(yu, 96, cols, yc, ys)
+            yu[16 * i : 16 * i + 16, cols] = twice(u) * y16
+        yu[96:112, cols] = y16
         store(
             yu, 112, cols, jnp.where(sub < 3, xc, jnp.where(sub < 6, xs, jnp.where(sub == 6, 1.0, 0.0))), zero
         )
         fb = feat_blk[:, cols].astype(F32)
         hot = jnp.broadcast_to(species_ref[0:1, cols], (8, CHUNK)) == sub
         sources = []
+        vc16, vs16 = twice(vc), twice(vs)
         for c in range(2):
             s = jnp.where(which[c], fb, 0.0) + jnp.where(hot, tabs[c], 0.0)
             s = jnp.broadcast_to(jnp.sum(s, axis=0, keepdims=True), (8, CHUNK))
             s = s.astype(BF16).astype(F32)
             sources.append(s)
             szc, szs = s * zc, s * zs
-            store(sz, 48 * c, cols, szc, szs)
-            store(sz, 48 * c + 16, cols, szc * vc, szs * vc)
-            store(sz, 48 * c + 32, cols, szc * vs, szs * vs)
+            s16 = jnp.concatenate([szc, szs], axis=0).astype(BF16)
+            sz[48 * c : 48 * c + 16, cols] = s16
+            sz[48 * c + 16 : 48 * c + 32, cols] = s16 * vc16
+            sz[48 * c + 32 : 48 * c + 48, cols] = s16 * vs16
         store(sz, 96, cols, jnp.where(sub < 3, sources[0], sources[1]) * ones, zero)
         return 0
 
@@ -275,10 +302,24 @@
         mil_copy(own_row, along_y(d), 1).start()
         return 0
 
-    lax.fori_loop(0, EARLY, gather_chunk, 0)
-    pl.semaphore_wait(barrier, nz - 1 + ny - 1 + n_atom - 1)
-    lax.fori_loop(0, nz - 1, send_z, 0)
-    lax.fori_loop(EARLY, n_chunks, gather_chunk, 0)
+    def gather(*accs):
+        def step(j, _):
+            multiply(accs, jnp.maximum(j - 1, 0))
+            gather_chunk(2 * j, 0)
+            gather_chunk(2 * j + 1, 0)
+            return 0
+
+        lax.fori_loop(0, EARLY, step, 0)
+        pl.semaphore_wait(barrier, nz - 1 + ny - 1 + n_atom - 1)
+        lax.fori_loop(0, nz - 1, send_z, 0)
+        lax.fori_loop(EARLY, n_chunks // 2, step, 0)
+        multiply(accs, n_chunks // 2 - 1)
+        gsend[...] = diagonal(accs)[0:GR, :].astype(BF16)
+
+    def accumulators(rows, times):
+        return [pltpu.ACC(i)((rows, 256), F32) for i in range(2) for _ in range(times)]
+
+    pl.run_scoped(gather, *accumulators(SR, 2))
 
     halves = ((0, SR, GR),)
 
@@ -305,23 +346,11 @@
             device_id_type=MESH,
         )
 
-    for half, (lo, up_to, hi) in enumerate(halves):
-
-        def add_products(j, _, lo=lo, up_to=up_to):
-            cols = pl.ds(pl.multiple_of(j * DEPTH, DEPTH), DEPTH)
-            gacc[lo:up_to, :] += lax.dot_general(
-                sz[lo:up_to, cols], yu[:, cols], (((1,), (1,)), ((), ())), preferred_element_type=F32
-            )
-            return 0
-
-        lax.fori_loop(0, atoms // DEPTH, add_products, 0)
-        gsend[lo:hi, :] = gacc[lo:hi, :].astype(BF16)
-
-        def send_g(i, _, half=half):
-            g_copy(half, ia, lax.rem(ia + 1 + lax.rem(i + 2, n_atom - 1), n_atom)).start()
-            return 0
-
-        lax.fori_loop(0, n_atom - 1, send_g, 0)
+    def send_g(i, _):
+        g_copy(0, ia, lax.rem(ia + 1 + lax.rem(i + 2, n_atom - 1), n_atom)).start()
+        return 0
+
+    lax.fori_loop(0, n_atom - 1, send_g, 0)
 
     for copy in loads[5:]:
         copy.wait()
@@ -363,31 +392,59 @@
     codes = jnp.where(used, a_r * 9 + q_r, -1).astype(F32)
     b_sub = jnp.where(third == 0, 0.0, 1.0)
     b_sub = jnp.where(sub < 6, b_sub, -1.0)
-    counts = jnp.zeros((128, LW), F32)
-    for j in range(n_vec // CHUNK):
-        m = mil_all[:, CHUNK * j : CHUNK * (j + 1)].astype(F32)
-        mx, my, mz = [jnp.broadcast_to(m[i : i + 1, :], (8, CHUNK)) for i in range(3)]
-        ma = jnp.round(mx * (1.0 / 3.0))
-        mb = mx - 3.0 * ma
-        ga, gb, gy, gz = [jnp.where(v < 0, -1.0, 1.0) for v in (ma, mb, my, mz)]
-        code = jnp.abs(ma) * 9.0 + jnp.abs(my)
-        hot_uy = jnp.where(codes == jnp.broadcast_to(code[0:1, :], (LW, CHUNK)), 1.0, 0.0).astype(BF16)
-        ab, ar, br, aq, bq, qr = ga * gb, ga * gz, gb * gz, ga * gy, gb * gy, gy * gz
-        az, absb = jnp.abs(mz), jnp.abs(mb)
-        hz = jnp.where(az == orders, 1.0, 0.0)
-        h1 = hz * absb
-        h0 = hz - h1
-        hs = jnp.where((az == 0.0) & (absb == b_sub), 1.0, 0.0)
-        wr = jnp.concatenate(
-            [h1, h1 * ab, h1 * ar, h1 * br, h1 * aq, h1 * bq, h1 * qr, h1 * (ab * qr)]
-            + [h0, h0 * aq, h0 * ar, h0 * qr]
-            + [hs, hs * ab, hs * aq, hs * bq],
-            axis=0,
-        ).astype(BF16)
-        counts = counts + lax.dot_general(
-            wr, hot_uy, (((1,), (1,)), ((), ())), preferred_element_type=F32
-        )
+    def count(*accs):
+        for j in range(n_vec // CHUNK):
+            m = mil_all[:, CHUNK * j : CHUNK * (j + 1)].astype(F32)
+            mx, my, mz = [jnp.broadcast_to(m[i : i + 1, :], (8, CHUNK)) for i in range(3)]
+            ma = jnp.round(mx * (1.0 / 3.0))
+            mb = mx - 3.0 * ma
+            ga, gb, gy, gz = [jnp.where(v < 0, -1.0, 1.0) for v in (ma, mb, my, mz)]
+            code = jnp.abs(ma) * 9.0 + jnp.abs(my)
+            hot_uy = jnp.where(codes == jnp.broadcast_to(code[0:1, :], (LW, CHUNK)), 1.0, 0.0).astype(BF16)
+            ab, ar, br, aq, bq, qr = ga * gb, ga * gz, gb * gz, ga * gy, gb * gy, gy * gz
+            az, absb = jnp.abs(mz), jnp.abs(mb)
+            hz = jnp.where(az == orders, 1.0, 0.0)
+            h1 = hz * absb
+            h0 = hz - h1
+            hs = jnp.where((az == 0.0) & (absb == b_sub), 1.0, 0.0)
+            wr = jnp.concatenate(
+                [h1, h1 * ab, h1 * ar, h1 * br, h1 * aq, h1 * bq, h1 * qr, h1 * (ab * qr)]
+                + [h0, h0 * aq, h0 * ar, h0 * qr]
+                + [hs, hs * ab, hs * aq, hs * bq],
+                axis=0,
+            ).astype(BF16)
+            pltpu.matmul_push_rhs(
+                jnp.concatenate([hot_uy[:, 0:256], hot_uy[:, 256:512]], axis=0), (j // 2) % 2, j % 2, transpose=True
+            )
+            pltpu.matmul_acc_lhs(accs[2 * (j % 2)], wr[:, 0:256], load_staged_rhs=(j // 2) % 2)
+            pltpu.matmul_acc_lhs(accs[2 * (j % 2) + 1], wr[:, 256:512])
+        counts_ref[...] = diagonal(accs)
+
+    pl.run_scoped(count, *accumulators(128, 2))
+    counts = counts_ref[...]
     w = [counts[8 * i : 8 * i + 8, :] for i in range(16)]
+
+    def mixed(plus, minus, plain, crossed):
+        half_s, half_d = 0.5 * (plus + minus), 0.5 * (plus - minus)
+        return half_s * plain + half_d * crossed, half_s * crossed + half_d * plain
+
+    same_uy = tu == ty
+    plain, coefs = [], []
+    for t in range(2):
+        plain.append((w[8], signed(same_uy, w[9]), signed(tu == t, w[10]), signed(ty == t, w[11])))
+    for c in range(2):
+        c_0, c_ab = mixed(rad_p[c], rad_m[c], w[0], w[1])
+        c_ar, c_br = mixed(rad_p[c], rad_m[c], w[2], w[3])
+        c_aq, c_bq = mixed(rad_p[c], rad_m[c], w[4], w[5])
+        c_qr, c_all = mixed(rad_p[c], rad_m[c], w[6], w[7])
+        at = lambda types, x: [signed(types == t, x) for t in range(2)]
+        coefs.append(
+            (c_0, signed(same_uy, c_aq), at(tu, c_ar), at(ty, c_qr), at(tu, c_ab), at(ty, c_bq), c_br)
+            + ([signed(tu != ty, c_all), signed(same_uy, c_all)],)
+        )
+    s_0, s_ab = mixed(single_p, single_m, w[12], w[13])
+    s_aq, s_bq = mixed(single_p, single_m, w[14], w[15])
+    s_aq, s_ab, s_bq = signed(same_uy, s_aq), signed(tu == tv_row, s_ab), signed(ty == tv_row, s_bq)
 
     all_g(0).wait_recv()
     grecv[ia] = gsend[...]
@@ -395,11 +452,6 @@
     for i in range(1, n_atom):
         g = g + grecv[i].astype(F32)
 
-    def mixed(plus, minus, plain, crossed):
-        half_s, half_d = 0.5 * (plus + minus), 0.5 * (plus - minus)
-        return half_s * plain + half_d * crossed, half_s * crossed + half_d * plain
-
-    same_uy = tu == ty
     rows = []
     for c in range(2):
         gb = [[g[48 * c + 16 * v + 8 * t : 48 * c + 16 * v + 8 * t + 8, :] for t in range(2)] for v in range(3)]
@@ -407,31 +459,26 @@
         gy = [[swap_y(x) for x in pair] for pair in gb]
         guy = [[swap_u(x) for x in pair] for pair in gy]
         for t in range(2):
-            h = w[8] * gb[0][t] + signed(same_uy, w[9]) * guy[0][t]
-            h = h + signed(tu == t, w[10]) * gu[0][1 - t] + signed(ty == t, w[11]) * gy[0][1 - t]
+            p_0, p_aq, p_ar, p_qr = plain[t]
+            h = p_0 * gb[0][t] + p_aq * guy[0][t] + p_ar * gu[0][1 - t] + p_qr * gy[0][1 - t]
             rows.append(h * rad_0[c])
-        c_0, c_ab = mixed(rad_p[c], rad_m[c], w[0], w[1])
-        c_ar, c_br = mixed(rad_p[c], rad_m[c], w[2], w[3])
-        c_aq, c_bq = mixed(rad_p[c], rad_m[c], w[4], w[5])
-        c_qr, c_all = mixed(rad_p[c], rad_m[c], w[6], w[7])
+        c_0, c_aq, c_ar, c_qr, c_ab, c_bq, c_br, c_all = coefs[c]
         for v in (1, 2):
             tv, o = v - 1, 3 - v
             for t in range(2):
-                h = c_0 * gb[v][t] + signed(same_uy, c_aq) * guy[v][t]
-                h = h + signed(tu == t, c_ar) * gu[v][1 - t] + signed(ty == t, c_qr) * gy[v][1 - t]
-                h = h + signed(tu == tv, c_ab) * gu[o][t] + signed(ty == tv, c_bq) * gy[o][t]
-                h = h + (-c_br if tv == t else c_br) * gb[o][1 - t]
-                odd = same_uy if (tv + t) % 2 == 1 else tu != ty
-                rows.append(h + signed(odd, c_all) * guy[o][1 - t])
+                h = c_0 * gb[v][t] + c_aq * guy[v][t] + c_ar[t] * gu[v][1 - t] + c_qr[t] * gy[v][1 - t]
+                h = h + c_ab[tv] * gu[o][t] + c_bq[tv] * gy[o][t]
+                cross = c_br * gb[o][1 - t]
+                h = h - cross if tv == t else h + cross
+                rows.append(h + c_all[(tv + t) % 2] * guy[o][1 - t])
     g0 = g[96:104, :]
     over = jnp.where(third1 == 1, pltpu.roll(g0, 7, 0), pltpu.roll(g0, 1, 0))
     over = jnp.where(b_row > 0.0, over, 0.0)
-    c_0, c_ab = mixed(single_p, single_m, w[12], w[13])
-    c_aq, c_bq = mixed(single_p, single_m, w[14], w[15])
-    h = c_0 * g0 + signed(same_uy, c_aq) * swap_u(swap_y(g0))
-    h = h + signed(tu == tv_row, c_ab) * swap_u(over) + signed(ty == tv_row, c_bq) * swap_y(over)
+    h = s_0 * g0 + s_aq * swap_u(swap_y(g0)) + s_ab * swap_u(over) + s_bq * swap_y(over)
     rows += [h, jnp.zeros((8, LW), F32)]
-    hmat[...] = jnp.concatenate(rows, axis=0).astype(BF16)
+    h16 = jnp.concatenate(rows, axis=0).astype(BF16)
+    hmat[...] = jnp.concatenate([h16, jnp.zeros_like(h16)], axis=1)
+    hmat_b[...] = jnp.concatenate([jnp.zeros_like(h16), h16], axis=1)
 
     def m_copy(slot, to):
         return pltpu.make_async_remote_copy(
@@ -458,20 +505,33 @@
             parts += [s[:, 128 * i : 128 * (i + 1)] for i in range(CHUNK // 128)]
         return jnp.concatenate(parts, axis=0).astype(BF16)
 
-    def send_messages(i, _):
+    def send_messages(accs, i, _):
         to = [partner(GROUP * i + k) for k in range(GROUP)]
         cols = [pl.ds(pl.multiple_of(j * CHUNK, CHUNK), CHUNK) for j in to]
-        ds = [jnp.dot(hmat[...], yu[:, c], preferred_element_type=F32) for c in cols]
         for k in range(GROUP):
-            msgs[to[k]] = message_of(ds[k], cols[k])
+            pltpu.matmul_push_rhs(
+                jnp.concatenate([tile(yu, 2 * to[k]), tile(yu, 2 * to[k] + 1)], axis=0), k // 2, k % 2
+            )
+            pair = accs[4 * (k % 2) + 2 * (k // 2) : 4 * (k % 2) + 2 * (k // 2) + 2]
+            pltpu.matmul_acc_lhs(pair[0], hmat[...], load_staged_rhs=k // 2)
+            pltpu.matmul_acc_lhs(pair[1], hmat_b[...])
+        for k in range(GROUP):
+            pair = accs[4 * (k % 2) + 2 * (k // 2) : 4 * (k % 2) + 2 * (k // 2) + 2]
+            d = jnp.concatenate([pltpu.matmul_pop(v) for v in pair], axis=1)
+            msgs[to[k]] = message_of(d, cols[k])
 
             @pl.when(to[k] != ik)
             def _():
                 m_copy(ik, to[k]).start()
         return 0
 
-    lax.fori_loop(0, n_ka // GROUP, send_messages, 0)
+    def send_all(*accs):
+        lax.fori_loop(0, n_ka // GROUP, functools.partial(send_messages, accs), 0)
+
+    pl.run_scoped(send_all, *accumulators(SR, 4))
     mrecv[ik] = msgs[ik]
+    up_t = up_ref[...].astype(F32).T.astype(BF16)
+    up_pad[...] = jnp.concatenate([up_t, jnp.zeros((up_t.shape[0], 192), BF16)], axis=1)
     eye = iota((64, 64), 0) == iota((64, 64), 1)
     gain = jnp.sum(jnp.where(eye, jnp.broadcast_to(gain_ref[...], (64, 64)), 0.0), axis=1, keepdims=True)
 
@@ -493,11 +553,24 @@
     )
     mean_sq = jnp.sum(message * message, axis=0, keepdims=True) * (1.0 / 64.0)
     normed = (message * lax.rsqrt(mean_sq + 1e-06) * gain).astype(BF16)
-    hidden = lax.dot_general(up_ref[...], normed, (((0,), (0,)), ((), ())), preferred_element_type=F32)
-    hidden = (hidden / (1.0 + jnp.exp(-hidden))).astype(BF16)
-    update = jnp.dot(down_ref[...], hidden, preferred_element_type=F32)
-    out_ref[...] = (feat_loc[...].astype(F32) + update).astype(BF16)
-
+    normed = jnp.concatenate([normed, jnp.zeros((192, local), BF16)], axis=0)
+
+    def node_update(*accs):
+        for i in range(2):
+            pltpu.matmul_push_rhs(normed[:, 256 * i : 256 * i + 256], 0, i)
+            pltpu.matmul_acc_lhs(accs[2 * i], up_pad[...], load_staged_rhs=0)
+        for i in range(2):
+            half = 0.5 * pltpu.matmul_pop(accs[2 * i])
+            hidden = (half + half * jnp.tanh(half)).astype(BF16)
+            pltpu.matmul_push_rhs(hidden, 1, i)
+            pltpu.matmul_acc_lhs(accs[2 * i + 1], down_ref[...], load_staged_rhs=1)
+        for i in range(2):
+            part = slice(256 * i, 256 * i + 256)
+            out_ref[:, part] = (feat_loc[:, part].astype(F32) + pltpu.matmul_pop(accs[2 * i + 1])).astype(BF16)
+
+    pl.run_scoped(
+        node_update, *[pltpu.ACC(i)((n, 256), F32) for i in range(2) for n in (up_pad.shape[0], 64)]
+    )
     all_z.wait_send()
     all_y.wait_send()
     all_messages().wait_send()
@@ -531,17 +604,19 @@
                 pltpu.VMEM((channels, hid), BF16),
                 pltpu.VMEM((8, atoms), BF16),
                 pltpu.VMEM((channels, local), BF16),
-                pltpu.VMEM((LW, atoms), BF16),
-                pltpu.VMEM((SR, atoms), BF16),
-                pltpu.VMEM((16, atoms), F32),
-                pltpu.VMEM((16, atoms), F32),
-                pltpu.VMEM((8, atoms), F32),
+                pltpu.VMEM((LW, atoms + PAD), BF16),
+                pltpu.VMEM((SR, atoms + PAD), BF16),
+                pltpu.VMEM((16, atoms + PAD), F32),
+                pltpu.VMEM((16, atoms + PAD), F32),
+                pltpu.VMEM((8, atoms + PAD), F32),
                 pltpu.VMEM((16, CHUNK), F32),
-                pltpu.VMEM((SR, LW), F32),
+                pltpu.VMEM((128, LW), F32),
+                pltpu.VMEM((hid, 256), BF16),
+                pltpu.VMEM((SR, 256), BF16),
                 pltpu.VMEM((GR, LW), BF16),
                 pltpu.VMEM((n_atom, GR, LW), BF16),
                 pltpu.VMEM((8, n_vectors), BF16),
-                pltpu.VMEM((SR, LW), BF16),
+                pltpu.VMEM((SR, 256), BF16),
                 pltpu.VMEM((n_ka, 8, 128), BF16),
                 pltpu.VMEM((n_ka, 8, 128), BF16),
                 pltpu.VMEM((n_ka * 8, 128), F32),

time: 25 us -> 25 us (level)
  no operation moved by 1% of the time
where the time goes in v7:
time: 25 us; the launch traced here: 24.9 us
  Pallas kernels  24.3 us (97%)
  local copies, waits for them, and re-layouts  0.63 us (3%)
    pallas_call x1, Pallas kernels, body(): pl.pallas_call(functools.partial(body_kernel, (n_atom, n_ka, ny, nz, atom...  24.3 us
    unnamed x1, local copies, waits for them, and re-layouts  0.63 us

profile of v7, /device:TPU:1, one launch (start us, length us, event | category | flops | bytes accessed | tf_op | source)
XLA Modules:
  0.0 24.9 jit_solution(1243975839910892137)
XLA Ops:
  0.0 24.3 %ewald.1 = bf16[64,512]{1,0:T(8,128)(2,1)S(1)} custom-call(f32[3,16384]{1,0:T(4,128)} %pos_hbm.1, bf16[64,16384]{1,0:T(8,128)(2,1)} %feat_hbm.1, s32[1,16384]{1,0:T(1,128)} %bitcast.5, s32[3,128]{1,0:T(4,128)} %miller_hbm.1, f32[8,64]{1,0:T(8,128)} %bitcast.8, f32[16,64]{1,0:T(8,128)} %bitcast.7, f32[1,64]{1,0:T(1,128)} %bitcast.9, bf16[64,256]{1,0:T(8,128)(2,1)} %bitcast.6, ...), custom_call_target="tpu_custom_call" | custom-call | tf_op jit(solution)/shard_map/ewald/pallas_call | solution.py:591
  24.3 0.6 %copy.11 = bf16[64,512]{1,0:T(8,128)(2,1)} copy(bf16[64,512]{1,0:T(8,128)(2,1)S(1)} %ewald.1) | data formatting | bytes 131072

commit v8 on v7

--- a/solution.py
+++ b/solution.py
@@ -83,7 +83,6 @@
     return jnp.where(same, -w, w)
 
 
-GROUP = 4
 PAD = 128
 
 
@@ -216,11 +215,14 @@
     def tile(ref, j):
         return ref[:, pl.ds(pl.multiple_of(j * 256, 256), 256)]
 
-    def multiply(accs, j):
+    def push(j):
         for i in range(2):
             pltpu.matmul_push_rhs(
                 jnp.concatenate([tile(yu, 4 * j + 2 * i), tile(yu, 4 * j + 2 * i + 1)], axis=0), 0, i, transpose=True
             )
+
+    def multiply(accs, j):
+        for i in range(2):
             pltpu.matmul_acc_lhs(accs[2 * i], tile(sz, 4 * j + 2 * i), load_staged_rhs=0)
             pltpu.matmul_acc_lhs(accs[2 * i + 1], tile(sz, 4 * j + 2 * i + 1))
 
@@ -241,7 +243,6 @@
         ones = jnp.where(third == 1, vc, jnp.where(third == 2, vs, 1.0))
         ones = jnp.where(sub < 6, ones, 0.0)
         zero = jnp.zeros((8, CHUNK), F32)
-        y16 = jnp.concatenate([yc, ys], axis=0).astype(BF16)
         zz[0:8, cols] = zc
         zz[8:16, cols] = zs
         vb[0:8, cols] = vc
@@ -249,8 +250,8 @@
         vv[:, cols] = ones
         for i, r in enumerate((0, 1, 2, 11, 12, 13)):
             u = row_of(r)
-            yu[16 * i : 16 * i + 16, cols] = twice(u) * y16
-        yu[96:112, cols] = y16
+            store(yu, 16 * i, cols, u * yc, u * ys)
+        store(yu, 96, cols, yc, ys)
         store(
             yu, 112, cols, jnp.where(sub < 3, xc, jnp.where(sub < 6, xs, jnp.where(sub == 6, 1.0, 0.0))), zero
         )
@@ -289,11 +290,6 @@
     def farther(k, n):
         return n // 2 + (1 - 2 * lax.rem(k, 2)) * ((k + 1) // 2)
 
-    def partner(i):
-        dz, dy = farther(i // ny, nz), farther(lax.rem(i, ny), ny)
-        y, z = lax.rem(ik // nz + dy, ny), lax.rem(lax.rem(ik, nz) + dz, nz)
-        return y * nz + z
-
     def send_z(i, _):
         mil_copy(own, along_z(farther(i, nz)), 0).start()
         return 0
@@ -304,6 +300,7 @@
 
     def gather(*accs):
         def step(j, _):
+            push(jnp.maximum(j - 1, 0))
             multiply(accs, jnp.maximum(j - 1, 0))
             gather_chunk(2 * j, 0)
             gather_chunk(2 * j + 1, 0)
@@ -313,6 +310,7 @@
         pl.semaphore_wait(barrier, nz - 1 + ny - 1 + n_atom - 1)
         lax.fori_loop(0, nz - 1, send_z, 0)
         lax.fori_loop(EARLY, n_chunks // 2, step, 0)
+        push(n_chunks // 2 - 1)
         multiply(accs, n_chunks // 2 - 1)
         gsend[...] = diagonal(accs)[0:GR, :].astype(BF16)
 
@@ -505,28 +503,41 @@
             parts += [s[:, 128 * i : 128 * (i + 1)] for i in range(CHUNK // 128)]
         return jnp.concatenate(parts, axis=0).astype(BF16)
 
-    def send_messages(accs, i, _):
-        to = [partner(GROUP * i + k) for k in range(GROUP)]
-        cols = [pl.ds(pl.multiple_of(j * CHUNK, CHUNK), CHUNK) for j in to]
-        for k in range(GROUP):
-            pltpu.matmul_push_rhs(
-                jnp.concatenate([tile(yu, 2 * to[k]), tile(yu, 2 * to[k] + 1)], axis=0), k // 2, k % 2
-            )
-            pair = accs[4 * (k % 2) + 2 * (k // 2) : 4 * (k % 2) + 2 * (k // 2) + 2]
-            pltpu.matmul_acc_lhs(pair[0], hmat[...], load_staged_rhs=k // 2)
-            pltpu.matmul_acc_lhs(pair[1], hmat_b[...])
-        for k in range(GROUP):
-            pair = accs[4 * (k % 2) + 2 * (k // 2) : 4 * (k % 2) + 2 * (k // 2) + 2]
-            d = jnp.concatenate([pltpu.matmul_pop(v) for v in pair], axis=1)
-            msgs[to[k]] = message_of(d, cols[k])
-
-            @pl.when(to[k] != ik)
-            def _():
-                m_copy(ik, to[k]).start()
-        return 0
+    def pair_of(accs, k):
+        return accs[4 * (k % 2) + 2 * (k // 2) : 4 * (k % 2) + 2 * (k // 2) + 2]
+
+    def issue(accs, k, j):
+        pltpu.matmul_push_rhs(jnp.concatenate([tile(yu, 2 * j), tile(yu, 2 * j + 1)], axis=0), k // 2, k % 2)
+        pair = pair_of(accs, k)
+        pltpu.matmul_acc_lhs(pair[0], hmat[...], load_staged_rhs=k // 2)
+        pltpu.matmul_acc_lhs(pair[1], hmat_b[...])
+
+    y_rows = [lax.rem(iy + ny // 2 + (k + 1) // 2 * (1 - 2 * (k % 2)), ny) * nz for k in range(ny)]
+
+    def z_of(i):
+        return lax.rem(iz + farther(i, nz), nz)
+
+    def send_group(accs, z, following):
+        for k in range(ny):
+            j = y_rows[k] + z
+            d = jnp.concatenate([pltpu.matmul_pop(v) for v in pair_of(accs, k)], axis=1)
+            if following is not None:
+                issue(accs, k, y_rows[k] + following)
+            msgs[j] = message_of(d, pl.ds(pl.multiple_of(j * CHUNK, CHUNK), CHUNK))
+            if following is not None or k < ny - 1:
+                m_copy(ik, j).start()
 
     def send_all(*accs):
-        lax.fori_loop(0, n_ka // GROUP, functools.partial(send_messages, accs), 0)
+        first = z_of(0)
+        for k in range(ny):
+            issue(accs, k, y_rows[k] + first)
+
+        def step(i, z):
+            following = z_of(i + 1)
+            send_group(accs, z, following)
+            return following
+
+        send_group(accs, lax.fori_loop(0, nz - 1, step, first), None)
 
     pl.run_scoped(send_all, *accumulators(SR, 4))
     mrecv[ik] = msgs[ik]

time: 25 us -> 25.2 us (level)
  no operation moved by 1% of the time
where the time goes in v8:
time: 25.2 us; the launch traced here: 25.1 us
  Pallas kernels  24.4 us (97%)
  local copies, waits for them, and re-layouts  0.63 us (2%)
    pallas_call x1, Pallas kernels, body(): pl.pallas_call(functools.partial(body_kernel, (n_atom, n_ka, ny, nz, atom...  24.4 us
    unnamed x1, local copies, waits for them, and re-layouts  0.63 us

profile of v8, /device:TPU:1, one launch (start us, length us, event | category | flops | bytes accessed | tf_op | source)
XLA Modules:
  0.0 25.1 jit_solution(5247190944744778480)
XLA Ops:
  0.0 24.4 %ewald.1 = bf16[64,512]{1,0:T(8,128)(2,1)S(1)} custom-call(f32[3,16384]{1,0:T(4,128)} %pos_hbm.1, bf16[64,16384]{1,0:T(8,128)(2,1)} %feat_hbm.1, s32[1,16384]{1,0:T(1,128)} %bitcast.5, s32[3,128]{1,0:T(4,128)} %miller_hbm.1, f32[8,64]{1,0:T(8,128)} %bitcast.8, f32[16,64]{1,0:T(8,128)} %bitcast.7, f32[1,64]{1,0:T(1,128)} %bitcast.9, bf16[64,256]{1,0:T(8,128)(2,1)} %bitcast.6, ...), custom_call_target="tpu_custom_call" | custom-call | tf_op jit(solution)/shard_map/ewald/pallas_call | solution.py:602
  24.4 0.6 %copy.11 = bf16[64,512]{1,0:T(8,128)(2,1)} copy(bf16[64,512]{1,0:T(8,128)(2,1)S(1)} %ewald.1) | data formatting | bytes 131072

commit v9 on v6

--- a/solution.py
+++ b/solution.py
@@ -18,7 +18,7 @@
 GR = 104
 CHUNK = 512
 DEPTH = 8192
-EARLY = 14
+EARLY = 12
 K_CUTOFF = 14.0
 
 def _fit():
@@ -84,7 +84,7 @@
     return jnp.where(same, -w, w)
 
 
-GROUP = 4
+PAD = 128
 
 
 def body_kernel(
@@ -262,11 +262,6 @@
     def farther(k, n):
         return n // 2 + (1 - 2 * lax.rem(k, 2)) * ((k + 1) // 2)
 
-    def partner(i):
-        dz, dy = farther(i // ny, nz), farther(lax.rem(i, ny), ny)
-        y, z = lax.rem(ik // nz + dy, ny), lax.rem(lax.rem(ik, nz) + dz, nz)
-        return y * nz + z
-
     def send_z(i, _):
         mil_copy(own, along_z(farther(i, nz)), 0).start()
         return 0
@@ -389,17 +384,34 @@
         )
     w = [counts[8 * i : 8 * i + 8, :] for i in range(16)]
 
+    def mixed(plus, minus, plain, crossed):
+        half_s, half_d = 0.5 * (plus + minus), 0.5 * (plus - minus)
+        return half_s * plain + half_d * crossed, half_s * crossed + half_d * plain
+
+    same_uy = tu == ty
+    plain, coefs = [], []
+    for t in range(2):
+        plain.append((w[8], signed(same_uy, w[9]), signed(tu == t, w[10]), signed(ty == t, w[11])))
+    for c in range(2):
+        c_0, c_ab = mixed(rad_p[c], rad_m[c], w[0], w[1])
+        c_ar, c_br = mixed(rad_p[c], rad_m[c], w[2], w[3])
+        c_aq, c_bq = mixed(rad_p[c], rad_m[c], w[4], w[5])
+        c_qr, c_all = mixed(rad_p[c], rad_m[c], w[6], w[7])
+        at = lambda types, x: [signed(types == t, x) for t in range(2)]
+        coefs.append(
+            (c_0, signed(same_uy, c_aq), at(tu, c_ar), at(ty, c_qr), at(tu, c_ab), at(ty, c_bq), c_br)
+            + ([signed(tu != ty, c_all), signed(same_uy, c_all)],)
+        )
+    s_0, s_ab = mixed(single_p, single_m, w[12], w[13])
+    s_aq, s_bq = mixed(single_p, single_m, w[14], w[15])
+    s_aq, s_ab, s_bq = signed(same_uy, s_aq), signed(tu == tv_row, s_ab), signed(ty == tv_row, s_bq)
+
     all_g(0).wait_recv()
     grecv[ia] = gsend[...]
     g = grecv[0].astype(F32)
     for i in range(1, n_atom):
         g = g + grecv[i].astype(F32)
 
-    def mixed(plus, minus, plain, crossed):
-        half_s, half_d = 0.5 * (plus + minus), 0.5 * (plus - minus)
-        return half_s * plain + half_d * crossed, half_s * crossed + half_d * plain
-
-    same_uy = tu == ty
     rows = []
     for c in range(2):
         gb = [[g[48 * c + 16 * v + 8 * t : 48 * c + 16 * v + 8 * t + 8, :] for t in range(2)] for v in range(3)]
@@ -407,29 +419,22 @@
         gy = [[swap_y(x) for x in pair] for pair in gb]
         guy = [[swap_u(x) for x in pair] for pair in gy]
         for t in range(2):
-            h = w[8] * gb[0][t] + signed(same_uy, w[9]) * guy[0][t]
-            h = h + signed(tu == t, w[10]) * gu[0][1 - t] + signed(ty == t, w[11]) * gy[0][1 - t]
+            p_0, p_aq, p_ar, p_qr = plain[t]
+            h = p_0 * gb[0][t] + p_aq * guy[0][t] + p_ar * gu[0][1 - t] + p_qr * gy[0][1 - t]
             rows.append(h * rad_0[c])
-        c_0, c_ab = mixed(rad_p[c], rad_m[c], w[0], w[1])
-        c_ar, c_br = mixed(rad_p[c], rad_m[c], w[2], w[3])
-        c_aq, c_bq = mixed(rad_p[c], rad_m[c], w[4], w[5])
-        c_qr, c_all = mixed(rad_p[c], rad_m[c], w[6], w[7])
+        c_0, c_aq, c_ar, c_qr, c_ab, c_bq, c_br, c_all = coefs[c]
         for v in (1, 2):
             tv, o = v - 1, 3 - v
             for t in range(2):
-                h = c_0 * gb[v][t] + signed(same_uy, c_aq) * guy[v][t]
-                h = h + signed(tu == t, c_ar) * gu[v][1 - t] + signed(ty == t, c_qr) * gy[v][1 - t]
-                h = h + signed(tu == tv, c_ab) * gu[o][t] + signed(ty == tv, c_bq) * gy[o][t]
-                h = h + (-c_br if tv == t else c_br) * gb[o][1 - t]
-                odd = same_uy if (tv + t) % 2 == 1 else tu != ty
-                rows.append(h + signed(odd, c_all) * guy[o][1 - t])
+                h = c_0 * gb[v][t] + c_aq * guy[v][t] + c_ar[t] * gu[v][1 - t] + c_qr[t] * gy[v][1 - t]
+                h = h + c_ab[tv] * gu[o][t] + c_bq[tv] * gy[o][t]
+                cross = c_br * gb[o][1 - t]
+                h = h - cross if tv == t else h + cross
+                rows.append(h + c_all[(tv + t) % 2] * guy[o][1 - t])
     g0 = g[96:104, :]
     over = jnp.where(third1 == 1, pltpu.roll(g0, 7, 0), pltpu.roll(g0, 1, 0))
     over = jnp.where(b_row > 0.0, over, 0.0)
-    c_0, c_ab = mixed(single_p, single_m, w[12], w[13])
-    c_aq, c_bq = mixed(single_p, single_m, w[14], w[15])
-    h = c_0 * g0 + signed(same_uy, c_aq) * swap_u(swap_y(g0))
-    h = h + signed(tu == tv_row, c_ab) * swap_u(over) + signed(ty == tv_row, c_bq) * swap_y(over)
+    h = s_0 * g0 + s_aq * swap_u(swap_y(g0)) + s_ab * swap_u(over) + s_bq * swap_y(over)
     rows += [h, jnp.zeros((8, LW), F32)]
     hmat[...] = jnp.concatenate(rows, axis=0).astype(BF16)
 
@@ -458,19 +463,24 @@
             parts += [s[:, 128 * i : 128 * (i + 1)] for i in range(CHUNK // 128)]
         return jnp.concatenate(parts, axis=0).astype(BF16)
 
-    def send_messages(i, _):
-        to = [partner(GROUP * i + k) for k in range(GROUP)]
+    y_rows = [lax.rem(iy + ny // 2 + (k + 1) // 2 * (1 - 2 * (k % 2)), ny) * nz for k in range(ny)]
+
+    def send_messages(i, last):
+        z = lax.rem(iz + farther(i, nz), nz)
+        to = [y + z for y in y_rows]
         cols = [pl.ds(pl.multiple_of(j * CHUNK, CHUNK), CHUNK) for j in to]
         ds = [jnp.dot(hmat[...], yu[:, c], preferred_element_type=F32) for c in cols]
-        for k in range(GROUP):
+        for k in range(ny):
             msgs[to[k]] = message_of(ds[k], cols[k])
-
-            @pl.when(to[k] != ik)
-            def _():
+            if last is None or k < ny - 1:
                 m_copy(ik, to[k]).start()
-        return 0
-
-    lax.fori_loop(0, n_ka // GROUP, send_messages, 0)
+
+    def send_step(i, _):
+        send_messages(i, None)
+        return 0
+
+    lax.fori_loop(0, nz - 1, send_step, 0)
+    send_messages(nz - 1, True)
     mrecv[ik] = msgs[ik]
     eye = iota((64, 64), 0) == iota((64, 64), 1)
     gain = jnp.sum(jnp.where(eye, jnp.broadcast_to(gain_ref[...], (64, 64)), 0.0), axis=1, keepdims=True)
@@ -494,7 +504,8 @@
     mean_sq = jnp.sum(message * message, axis=0, keepdims=True) * (1.0 / 64.0)
     normed = (message * lax.rsqrt(mean_sq + 1e-06) * gain).astype(BF16)
     hidden = lax.dot_general(up_ref[...], normed, (((0,), (0,)), ((), ())), preferred_element_type=F32)
-    hidden = (hidden / (1.0 + jnp.exp(-hidden))).astype(BF16)
+    half = 0.5 * hidden
+    hidden = (half + half * jnp.tanh(half)).astype(BF16)
     update = jnp.dot(down_ref[...], hidden, preferred_element_type=F32)
     out_ref[...] = (feat_loc[...].astype(F32) + update).astype(BF16)
 
@@ -531,11 +542,11 @@
                 pltpu.VMEM((channels, hid), BF16),
                 pltpu.VMEM((8, atoms), BF16),
                 pltpu.VMEM((channels, local), BF16),
-                pltpu.VMEM((LW, atoms), BF16),
-                pltpu.VMEM((SR, atoms), BF16),
-                pltpu.VMEM((16, atoms), F32),
-                pltpu.VMEM((16, atoms), F32),
-                pltpu.VMEM((8, atoms), F32),
+                pltpu.VMEM((LW, atoms + PAD), BF16),
+                pltpu.VMEM((SR, atoms + PAD), BF16),
+                pltpu.VMEM((16, atoms + PAD), F32),
+                pltpu.VMEM((16, atoms + PAD), F32),
+                pltpu.VMEM((8, atoms + PAD), F32),
                 pltpu.VMEM((16, CHUNK), F32),
                 pltpu.VMEM((SR, LW), F32),
                 pltpu.VMEM((GR, LW), BF16),

time: 25 us -> 24.9 us (level)
  no operation moved by 1% of the time
where the time goes in v9:
time: 24.9 us; the launch traced here: 24.8 us
  Pallas kernels  24.2 us (97%)
  local copies, waits for them, and re-layouts  0.63 us (3%)
    pallas_call x1, Pallas kernels, body(): pl.pallas_call(functools.partial(body_kernel, (n_atom, n_ka, ny, nz, atom...  24.2 us
    unnamed x1, local copies, waits for them, and re-layouts  0.63 us

profile of v9, /device:TPU:1, one launch (start us, length us, event | category | flops | bytes accessed | tf_op | source)
XLA Modules:
  0.0 24.8 jit_solution(2619442670978369965)
XLA Ops:
  0.0 24.2 %ewald.1 = bf16[64,512]{1,0:T(8,128)(2,1)S(1)} custom-call(f32[3,16384]{1,0:T(4,128)} %pos_hbm.1, bf16[64,16384]{1,0:T(8,128)(2,1)} %feat_hbm.1, s32[1,16384]{1,0:T(1,128)} %bitcast.5, s32[3,128]{1,0:T(4,128)} %miller_hbm.1, f32[8,64]{1,0:T(8,128)} %bitcast.8, f32[16,64]{1,0:T(8,128)} %bitcast.7, f32[1,64]{1,0:T(1,128)} %bitcast.9, bf16[64,256]{1,0:T(8,128)(2,1)} %bitcast.6, ...), custom_call_target="tpu_custom_call" | custom-call | tf_op jit(solution)/shard_map/ewald/pallas_call | solution.py:529
  24.2 0.6 %copy.11 = bf16[64,512]{1,0:T(8,128)(2,1)} copy(bf16[64,512]{1,0:T(8,128)(2,1)S(1)} %ewald.1) | data formatting | bytes 131072
